TPU v7x, 32 devices: a whole 2x2x4 slice. The times are simulated.
32 devices in a mesh: fsdp: 4 (over y, x), heads: 2 (over core), tensor: 4 (over z).
Axes of the slice: x: 2, y: 2, z: 4, core: 2. Of those that a mesh axis runs over, the one named last changes fastest.
Arguments:
- inputs: float32 [32, 729, 1152], P(('fsdp', 'heads', 'tensor')), may hold values from -6 to 6
- cotangent: float32 [32, 729, 1152], P(('fsdp', 'heads', 'tensor')), may hold values from -6 to 6
- image_adapter_index: int32 [32], replicated, may hold values from 0 to 7
- first_norm_gain: float32 [1152], replicated, may hold values from 0.5 to 1.5
- first_norm_bias: float32 [1152], replicated, may hold values from -3 to 3
- second_norm_gain: float32 [1152], replicated, may hold values from 0.5 to 1.5
- second_norm_bias: float32 [1152], replicated, may hold values from -3 to 3
- query_key_value_weight: bfloat16 [1152, 3, 1152], P('fsdp', None, 'heads'), may hold values from -0.1875 to 0.1875
- attention_output_weight: bfloat16 [1152, 1152], P('fsdp', 'heads'), may hold values from -3 to 3
- up_weight: bfloat16 [1152, 4304], P('fsdp', 'tensor'), may hold values from -0.1875 to 0.1875
- down_weight: bfloat16 [1152, 4304], P('fsdp', 'tensor'), may hold values from -0.09375 to 0.09375
- up_projection_bias: bfloat16 [4304], P('tensor'), may hold values from -3 to 3
- down_projection_bias: bfloat16 [1152], replicated, may hold values from -3 to 3
- query_key_value_adapter_first: bfloat16 [3, 8, 1152, 16], replicated, may hold values from -0.1875 to 0.1875
- query_key_value_adapter_second: bfloat16 [3, 8, 16, 1152], P(None, None, None, 'heads'), may hold values from -0.75 to 0.75
- projection_adapter_first: bfloat16 [8, 1152, 16], P(None, 'heads'), may hold values from -3 to 3
- projection_adapter_second: bfloat16 [8, 16, 1152], replicated, may hold values from -0.75 to 0.75
- up_adapter_first: bfloat16 [8, 1152, 16], replicated, may hold values from -0.1875 to 0.1875
- up_adapter_second: bfloat16 [8, 16, 4304], P(None, None, 'tensor'), may hold values from -0.75 to 0.75
- down_adapter_first: bfloat16 [8, 16, 4304], P(None, None, 'tensor'), may hold values from -0.09375 to 0.09375
- down_adapter_second: bfloat16 [8, 16, 1152], replicated, may hold values from -0.75 to 0.75
Outputs:
- layer_output: float32 [32, 729, 1152], P(('fsdp', 'heads', 'tensor'))
- grad_input: float32 [32, 729, 1152], P(('fsdp', 'heads', 'tensor'))
- grad_qkv_in: float32 [3, 8, 1152, 16], replicated
- grad_qkv_out: float32 [3, 8, 16, 1152], P(None, None, None, 'heads')
- grad_proj_in: float32 [8, 1152, 16], P(None, 'heads')
- grad_proj_out: float32 [8, 16, 1152], replicated
- grad_up_in: float32 [8, 1152, 16], replicated
- grad_up_out: float32 [8, 16, 4304], P(None, None, 'tensor')
- grad_down_in: float32 [8, 16, 4304], P(None, None, 'tensor')
- grad_down_out: float32 [8, 16, 1152], replicated
All inputs are finite; a program needn't handle non-finite values.
Results may differ from a plain program's by a relative error of at most 0.02.
Values may be sent and summed in bfloat16 or wider, within the bound.
A program may use at most 256 MiB of HBM per device.

v0:
```python
import functools
import jax
import jax.numpy as jnp
from jax import lax
from jax.experimental import pallas as pl
from jax.experimental.pallas import tpu as pltpu
from jax.sharding import PartitionSpec as P

HEAD_DIM = 72
norm_eps = 1e-06
f32 = jnp.float32
bf16 = jnp.bfloat16
MESH = pl.DeviceIdType.MESH


RANK = 16
EXTRA = 32


def padded(n):
    return -(-n // 16) * 16


def row_sums(v):
    return jnp.sum(v, axis=-1, keepdims=True)


class Tokens:
    def __init__(self, hbm, buf, tail, sems, out=False):
        self.length = hbm.shape[0]
        self.buf, self.tail, self.out = buf, tail, out
        self.whole = self.length // 8 * 8
        pairs = [(hbm.at[0 : self.whole, 0, :], buf.at[0 : self.whole, 0 : hbm.shape[-1]])]
        if self.whole < self.length:
            pairs.append((hbm.at[self.whole : self.length, 0, :], tail))
        self.copies = [
            pltpu.make_async_copy(*((b, a) if out else (a, b)), sems.at[i]) for i, (a, b) in enumerate(pairs)
        ]

    def start(self):
        if self.out and self.whole < self.length:
            self.tail[...] = self.buf[self.whole : self.length, 0 : self.tail.shape[-1]]
        for c in self.copies:
            c.start()

    def wait(self):
        for c in self.copies:
            c.wait()
        if not self.out:
            rest = self.buf.shape[0] - self.length
            zeros = jnp.zeros((rest, self.buf.shape[1]), f32)
            if self.whole < self.length:
                zeros = jnp.concatenate([self.tail[...], zeros])
            self.buf[self.whole :, :] = zeros


def tail_shape(length, width):
    return pltpu.VMEM((max(length % 8, 1), width), f32)


def unit_of(v, width):
    mean = row_sums(v) * (1.0 / width)
    centred = v - mean
    inverse = lax.rsqrt(row_sums(centred * centred) * (1.0 / width) + norm_eps)
    return centred * inverse, inverse


def by_rows(n, step, body):
    def one(r, _):
        body(pl.ds(pl.multiple_of(r * step, step), step), r * step)
        return 0

    lax.fori_loop(0, n // step, one, 0)


def real(v, start, length):
    row = lax.broadcasted_iota(jnp.int32, v.shape, 0) + start
    return jnp.where(row < length, v, 0.0)


def normalize_into(dst, src, gain, bias, length):
    n, width = src.shape

    def body(rows, start):
        unit, _ = unit_of(src[rows, :], width)
        dst[rows, 0:width] = real(unit * gain[...] + bias[...], start, length).astype(bf16)

    by_rows(n, 32, body)


def norm_back(grad, v, gain, width):
    unit, inverse = unit_of(v, width)
    e = grad * gain
    return inverse * (e - row_sums(e) * (1.0 / width) - unit * (row_sums(e * unit) * (1.0 / width)))


LANES = 128
SCALE = HEAD_DIM**-0.5
LOG2E = 1.4426950408889634


def nn(a, b):
    return lax.dot_general(a, b, (((1,), (0,)), ((), ())), preferred_element_type=f32)


def nt(a, b):
    return lax.dot_general(a, b, (((1,), (1,)), ((), ())), preferred_element_type=f32)


def tn_(a, b):
    return lax.dot_general(a, b, (((0,), (0,)), ((), ())), preferred_element_type=f32)


def whole(shape):
    return pl.BlockSpec(shape, lambda *_: (0,) * len(shape))


def params(limit=60, **more):
    return pltpu.CompilerParams(vmem_limit_bytes=limit << 20, **more)


def head_window(head, width):
    tile = jnp.minimum(head * HEAD_DIM // LANES, width // LANES - 2)
    return pl.ds(pl.multiple_of(tile * LANES, LANES), 2 * LANES), head * HEAD_DIM - tile * LANES


def only_head(values, start):
    lane = lax.broadcasted_iota(jnp.int32, values.shape, 1)
    return jnp.where((lane >= start) & (lane < start + HEAD_DIM), values, jnp.zeros_like(values))


def own_rows(head):
    return pl.ds(pl.multiple_of(head * HEAD_DIM, 8), HEAD_DIM)


def attend_forward_head(length, head, q_ref, k_ref, vt_ref, sum_ref, log_ref):
    win, start = head_window(head, q_ref.shape[-1])
    q = only_head(q_ref[:, win], start)
    v = vt_ref[own_rows(head), :].astype(bf16)
    s = nt(k_ref[:, win], q)
    key = lax.broadcasted_iota(jnp.int32, s.shape, 0)
    s = jnp.where(key < length, s, -1e30)
    top = jnp.max(s, axis=0, keepdims=True)
    p = jnp.exp2((s - top) * (SCALE * LOG2E))
    total = jnp.sum(p, axis=0, keepdims=True)
    sum_ref[own_rows(head), :] = nn(v, p.astype(bf16)) * (1.0 / total)
    log_ref[pl.ds(head, 1), :] = top * (SCALE * LOG2E) + jnp.log(total) * LOG2E


def attend_back_head(length, head, q_ref, k_ref, v_ref, do_ref, log_ref, kt_ref, dq_ref, dk_ref, dv_ref):
    win, start = head_window(head, q_ref.shape[-1])
    q = only_head(q_ref[:, win], start)
    k = k_ref[:, win]
    do = only_head(do_ref[:, win], start)
    s = nt(k, q)
    key = lax.broadcasted_iota(jnp.int32, s.shape, 0)
    p = jnp.exp2(jnp.where(key < length, s * (SCALE * LOG2E), -1e30) - log_ref[pl.ds(head, 1), :])
    dp = nt(v_ref[:, win], do)
    pd = p * dp
    ds = (pd - p * jnp.sum(pd, axis=0, keepdims=True)).astype(bf16)
    dv_ref[:, win] += nn(p.astype(bf16), do)
    dk_ref[:, win] += nn(ds, q) * SCALE
    dq_ref[own_rows(head), :] = nn(kt_ref[own_rows(head), :].astype(bf16), ds) * SCALE


def columns(width, body):
    def one(c, _):
        body(pl.ds(pl.multiple_of(c * LANES, LANES), LANES))
        return 0

    lax.fori_loop(0, width // LANES, one, 0)


def to_rows(dst, src):
    def body(at):
        dst[at, :] = src[:, at].astype(f32).T.astype(dst.dtype)

    columns(src.shape[1], body)


def to_lanes(dst, src):
    def body(at):
        dst[:, at] = src[at, :].T.astype(dst.dtype)

    columns(src.shape[0], body)


def bits_of(n):
    return n.bit_length() - 1


class Comm:
    def __init__(self, send, recv):
        self.send, self.recv, self.n = send, recv, 0

    def new(self):
        self.n += 1
        return self.n - 1

    def copy(self, i, src, dst, **where):
        return pltpu.make_async_remote_copy(
            src_ref=src,
            dst_ref=dst,
            send_sem=self.send.at[i],
            recv_sem=self.recv.at[i],
            device_id=where,
            device_id_type=MESH,
        )


def enter(axes_sizes, f, h, z):
    fn, hn, tn = axes_sizes
    barrier = pltpu.get_barrier_semaphore()
    count = 0
    for b in range(bits_of(fn)):
        pl.semaphore_signal(
            barrier, 1, device_id={"fsdp": f ^ (1 << b)}, device_id_type=MESH
        )
        count += 1
    pl.semaphore_signal(barrier, 1, device_id={"heads": 1 - h}, device_id_type=MESH)
    count += 1
    for d in range(1, tn):
        pl.semaphore_signal(
            barrier, 1, device_id={"tensor": lax.rem(z + d, tn)}, device_id_type=MESH
        )
        count += 1
    pl.semaphore_wait(barrier, count)


class Rows:
    def __init__(self, comm, fn, f, slot, rows, own, align=8):
        self.comm, self.fn, self.f, self.slot, self.own = comm, fn, f, slot, own
        self.nb = bits_of(fn)
        half = rows // 2 // align * align
        self.parts = ((0, half, list(range(self.nb))), (half, rows - half, list(range(self.nb))[::-1]))
        self.first = [comm.new() for _ in range(self.nb)]
        self.later = {}
        for p, (_, _, order) in enumerate(self.parts):
            for m in range(1, fn):
                last = max(order.index(b) for b in range(self.nb) if m >> b & 1)
                for b in order[last + 1 :]:
                    self.later[p, m, b] = comm.new()
        self.sent = []

    def part(self, origin, p):
        start, size, _ = self.parts[p]
        return self.slot(origin, (start, size))

    def begin(self):
        for b in range(self.nb):
            self.send(
                lambda b=b: self.comm.copy(
                    self.first[b], self.own(), self.slot(self.f, None), fsdp=self.f ^ (1 << b)
                )
            )

    def _arrived(self, m, p):
        order = self.parts[p][2]
        last = max(order.index(b) for b in range(self.nb) if m >> b & 1)
        b = order[last]
        src = m ^ (1 << b)
        if src == 0:
            return None
        where = self.part(self.f ^ m, p)
        return self.comm.copy(self.later[p, src, b], where, where, fsdp=self.f ^ (1 << b))

    def forward(self, m):
        if m & (m - 1) == 0:
            b = bits_of(m)
            where = self.slot(self.f ^ m, None)
            self.comm.copy(self.first[b], where, where, fsdp=self.f ^ m).wait_recv()
        for p, (_, _, order) in enumerate(self.parts):
            if m & (m - 1):
                self._arrived(m, p).wait_recv()
            last = max(order.index(b) for b in range(self.nb) if m >> b & 1)
            for b in order[last + 1 :]:

                def onward(p=p, b=b):
                    where = self.part(self.f ^ m, p)
                    return self.comm.copy(self.later[p, m, b], where, where, fsdp=self.f ^ (1 << b))

                self.send(onward)

    def masks(self):
        return sorted(range(1, self.fn), key=lambda m: (bin(m).count("1"), m))

    def leaf(self, m):
        return not any(key[1] == m for key in self.later)

    def forward_all(self):
        for m in self.masks():
            if not self.leaf(m):
                self.forward(m)

    def settle(self):
        for m in self.masks():
            if self.leaf(m):
                self.forward(m)

    def send(self, make):
        make().start()
        self.sent.append(make)

    def drain(self):
        for make in self.sent:
            make().wait_send()


def tree_sems(fn):
    nb = bits_of(fn)
    return nb + 2 * (fn - 1 - nb)


class Bounce:
    def __init__(self, src, buf, dst, sem):
        self.load = pltpu.make_async_copy(src, buf, sem)
        self.save = pltpu.make_async_copy(buf, dst, sem)

    def start(self):
        self.load.start()

    def turn(self):
        self.load.wait()
        self.save.start()

    def wait(self):
        self.save.wait()


class Block:
    def __init__(self, comm, sizes, zw, dst, s, buf, own=None):
        fn, hn, tn = sizes
        f, h, z = lax.axis_index("fsdp"), lax.axis_index("heads"), lax.axis_index("tensor")
        rows = zw.shape[1]
        self.comm, self.dst, self.h, self.buf = comm, dst, h, buf
        t = lax.rem(z + s, tn)

        def slot(o, r):
            start, size = (0, rows) if r is None else r
            return dst.at[h, pl.ds(pl.multiple_of(o * rows + start, 8), size)]

        self.own = lambda: zw.at[t] if own is None else own
        self.slot = lambda: slot(f, None)
        self.job = Rows(comm, fn, f, slot, rows, self.own)
        self.local = comm.new()
        self.core = comm.new()

    def mine(self):
        return Bounce(self.own(), self.buf, self.slot(), self.comm.send.at[self.local])

    def to_core(self, which):
        b = self.dst.at[which]
        return self.comm.copy(self.core, b, b, heads=1 - self.h)

    def begin(self):
        self.job.begin()
        self.mine().start()

    def forward(self):
        self.mine().turn()
        self.job.forward_all()

    def exchange(self):
        self.job.settle()
        self.mine().wait()
        self.to_core(self.h).start()

    def arrive(self):
        self.to_core(1 - self.h).wait_recv()

    def drain(self):
        self.job.drain()
        self.to_core(self.h).wait_send()


def block_sems(fn):
    return tree_sems(fn) + 2


class Weight:
    def __init__(self, comm, fn, f, h, rows, own, dst, extra, own_sem, buf):
        self.comm, self.h, self.dst, self.extra = comm, h, dst, extra
        width = fn * rows
        self.main, self.more = pl.ds(0, width), pl.ds(width, RANK)

        def slot(o, r):
            start, size = (0, rows) if r is None else r
            return dst.at[h, pl.ds(pl.multiple_of(o * rows + start, 8), size)]

        self.job = Rows(comm, fn, f, slot, rows, lambda: own)
        self.core, self.core_extra = comm.new(), comm.new()
        self.mine = lambda: Bounce(own, buf, slot(f, None), own_sem.at[0])
        self.mine_extra = lambda: pltpu.make_async_copy(
            extra.at[h], dst.at[h, self.more], own_sem.at[1]
        )

    def start_extra(self):
        self.mine_extra().start()
        self.to_core_extra().start()

    def to_core_extra(self):
        return self.comm.copy(
            self.core_extra, self.extra.at[1 - self.h], self.dst.at[self.h, self.more], heads=1 - self.h
        )

    def to_core(self, which):
        b = self.dst.at[which, self.main]
        return self.comm.copy(self.core, b, b, heads=1 - self.h)

    def exchange(self):
        self.job.settle()
        self.mine().wait()
        self.to_core(self.h).start()

    def arrive(self):
        self.mine_extra().wait()
        where = self.dst.at[1 - self.h, self.more]
        self.comm.copy(self.core_extra, where, where, heads=1 - self.h).wait_recv()
        self.to_core(1 - self.h).wait_recv()

    def drain(self):
        self.job.drain()
        self.to_core(self.h).wait_send()
        self.to_core_extra().wait_send()


def attention_kernel(
    sizes,
    wq,
    wo,
    wu,
    wd,
    bq,
    bp,
    bu,
    bd,
    ub,
    index,
    first_ref,
    out_ref,
    x_ref,
    vectors,
    up_ref,
    oq,
    oo,
    zw,
    ax,
    ln_out,
    qkv_out,
    qmid_ref,
    mixed_ref,
    log_ref,
    hidden_ref,
    ln2_ref,
    mid_ref,
    got,
    send,
    recv,
    wq_buf,
    wo_buf,
    w_sems,
    own_sems,
    own_q,
    own_o,
    own_z,
    own_b,
    aq,
    ap,
    a2,
    qkv_ref,
    lnx_ref,
    vt_ref,
    sum_ref,
    x_buf,
    x_tail,
    x_sems,
):
    i = pl.program_id(0)
    fn, hn, tn = sizes
    f, h, z = lax.axis_index("fsdp"), lax.axis_index("heads"), lax.axis_index("tensor")
    rows, half = wo.shape
    length = x_ref.shape[0]
    n, width = mixed_ref.shape
    number = index[(f * hn + h) * tn + z]
    gain1, bias1, gain, bias = (vectors.at[k : k + 1] for k in range(4))
    heads = width // HEAD_DIM
    comm = Comm(send, recv)
    qs = [
        Weight(comm, fn, f, h, rows, wq.at[j], oq.at[j], aq.at[j], own_sems.at[j], own_q.at[j])
        for j in range(3)
    ]
    o = Weight(comm, fn, f, h, rows, wo, oo, ap, own_sems.at[3], own_o)
    line = ([comm.new() for _ in range(tn - 1)], [comm.new() for _ in range(tn - 1)])
    small = [comm.new() for _ in range(tn - 1)]
    blocks = [
        Block(comm, sizes, zw, got.at[b], b, own_b.at[b], own_z if b == 0 else None)
        for b in range(got.shape[0])
    ]
    begin_z, step_z, drain_z = line_copies(comm, tn, z, lambda t: zw.at[t], line, own_z)
    mine_z = [Bounce(w, own_z, zw.at[z], own_sems.at[4, 0]) for w in (wu, wd)]
    mine_a = lambda: pltpu.make_async_copy(a2.at[z], ax.at[:, z], own_sems.at[4, 1])
    to_line = lambda d: comm.copy(
        small[d - 1], a2.at[lax.rem(z + d, tn)], ax.at[:, z], tensor=lax.rem(z + d, tn)
    )
    load_x = Tokens(x_ref, x_buf, x_tail, x_sems)
    load_q = lambda j: pltpu.make_async_copy(oq.at[j], wq_buf.at[j], w_sems.at[j])
    load_o = lambda: pltpu.make_async_copy(oo, wo_buf, w_sems.at[3])
    save_ln = lambda: pltpu.make_async_copy(lnx_ref.at[:, pl.ds(0, width)], ln_out, w_sems.at[4])
    save_qkv = lambda: pltpu.make_async_copy(qkv_ref, qkv_out, w_sems.at[5])

    @pl.when(i == 0)
    def _():
        load_x.start()
        for w in qs + [o]:
            w.mine().start()
        for p in range(2):

            @pl.when(h == p)
            def _():
                mine_z[p].start()

        for p in range(hn):
            k = index[(f * hn + p) * tn + z]
            for j in range(3):
                aq[j, p] = bq[j, k]
            ap[p] = bp[k]
        for t in range(tn):
            k = index[(f * hn + h) * tn + t]
            a2[t, 0, 0:RANK] = bu[k]
            a2[t, 1, 0:RANK] = bd[k]
            a2[t, 0, RANK:] = ub[...]
            a2[t, 1, RANK:] = jnp.zeros_like(ub)
        enter(sizes, f, h, z)
        qs[0].job.begin()
        qs[1].job.begin()
        mine_z[0].turn()
        begin_z()
        for w in qs + [o]:
            w.start_extra()
        mine_a().start()
        for d in range(1, tn):
            to_line(d).start()
        for w in qs + [o]:
            w.mine().turn()
        load_x.wait()
        normalize_into(lnx_ref, x_buf, gain1, bias1, length)
        save_ln().start()

    @pl.when(i == 1)
    def _():
        qs[0].job.forward_all()
        qs[2].job.begin()
        qs[1].job.forward_all()
        qs[0].exchange()
        step_z(0, lambda t: None)
        qs[0].arrive()
        load_q(0).start()

    @pl.when(i == 2)
    def _():
        qs[2].job.forward_all()
        o.job.begin()
        qs[1].exchange()
        if tn > 2:
            step_z(1, lambda t: None)
        qs[1].arrive()
        load_q(1).start()
        qs[2].exchange()

    @pl.when(i == 3)
    def _():
        qs[2].arrive()
        load_q(2).start()

    @pl.when((i >= 1) & (i < 4))
    def _():
        j = i - 1
        mid = nt(lnx_ref[:, 0:width], first_ref[j, number]).astype(bf16)
        qmid_ref[j] = mid
        load_q(j).wait()

        @pl.when(i == 1)
        def _():
            save_ln().wait()

        lnx_ref[:, width:] = mid
        for p in range(hn):
            qkv_ref[j, :, p * half : (p + 1) * half] = nn(lnx_ref[...], wq_buf[j, p]).astype(bf16)

    @pl.when(i == 4)
    def _():
        save_qkv().start()
        o.job.forward_all()
        blocks[0].begin()
        for k in range(2, tn - 1):
            step_z(k, lambda t: None)
        for b in blocks[1:]:
            b.begin()
        to_rows(vt_ref, qkv_ref.at[2])

    @pl.when(i == 8)
    def _():
        o.exchange()

    @pl.when(i == 11)
    def _():
        o.arrive()
        load_o().start()

    for b in range(got.shape[0]):

        @pl.when(i == 16 + 3 * b)
        def _():
            blocks[b].forward()

    @pl.when((i >= 4) & (i < 4 + heads))
    def _():
        attend_forward_head(length, i - 4, qkv_ref.at[0], qkv_ref.at[1], vt_ref, sum_ref, log_ref)

    @pl.when(i == 4 + heads)
    def _():
        blocks[0].exchange()
        to_lanes(mixed_ref, sum_ref)
        load_o().wait()
        br = sum(nt(mixed_ref[:, p * half : (p + 1) * half], wo_buf[p]) for p in range(hn))
        mid = br[:, width:].astype(bf16)
        mid_ref[...] = mid
        hidden_ref[...] = br[:, :width] + nn(mid, out_ref[number])

    @pl.when(i == 5 + heads)
    def _():
        for b in blocks[1:]:
            b.exchange()

        def body(rows, start):
            v = real(x_buf[rows, :] + hidden_ref[rows, :], start, length)
            hidden_ref[rows, :] = v
            unit, _ = unit_of(v, width)
            ln2_ref[rows, 0:width] = real(unit * gain[...] + bias[...], start, length).astype(bf16)

        by_rows(n, 32, body)
        up_mid = nt(ln2_ref[:, 0:width], up_ref[number])
        lane = lax.broadcasted_iota(jnp.int32, (n, EXTRA - RANK), 1)
        ln2_ref[:, width : width + RANK] = up_mid.astype(bf16)
        ln2_ref[:, width + RANK :] = (lane == 0).astype(bf16)
        save_qkv().wait()
        mine_z[0].wait()
        mine_a().wait()
        for d in range(1, tn):
            to_line(d).wait_send()
            p = lax.rem(z + tn - d, tn)
            comm.copy(small[d - 1], a2.at[p], ax.at[:, p], tensor=p).wait_recv()
        drain_z()
        for b in blocks:
            b.arrive()
        for w in qs + [o] + blocks:
            w.drain()


def attention(sizes, wq, wo, wu, wd, bq, bp, bu, bd, ub, index, first, out, x, vectors, up):
    fn, hn, tn = sizes
    rows, half = wo.shape
    units = wu.shape[-1]
    width = fn * rows
    length = x.shape[0]
    n = padded(length)
    heads = width // HEAD_DIM
    early = min(2, tn)
    any_ = pl.BlockSpec(memory_space=pl.ANY)
    one = lambda s: pl.BlockSpec(s, lambda i: (0,) * len(s), pipeline_mode=pl.Buffered(1))
    shape = jax.ShapeDtypeStruct
    nsem = 4 * (tree_sems(fn) + 2) + 3 * (tn - 1) + early * block_sems(fn)
    hbm = [
        ((3, hn, width + RANK, half), bf16),
        ((hn, width + RANK, half), bf16),
        ((tn, rows, units), bf16),
        ((2, tn, EXTRA, units), bf16),
        ((n, width), bf16),
        ((3, n, width), bf16),
    ]
    outs = [
        ((3, n, RANK), bf16),
        ((n, width), bf16),
        ((heads, n), f32),
        ((n, width), f32),
        ((n, width + EXTRA), bf16),
        ((n, RANK), bf16),
    ]
    return pl.pallas_call(
        functools.partial(attention_kernel, sizes),
        grid=(6 + heads,),
        in_specs=[any_] * 4
        + [one(v.shape) for v in (bq, bp, bu, bd, ub)]
        + [pl.BlockSpec(memory_space=pltpu.SMEM)]
        + [one(first.shape), one(out.shape), any_, one(vectors.shape), one(up.shape)],
        out_specs=(any_,) * len(hbm) + tuple(one(s) for s, _ in outs) + (any_,),
        out_shape=tuple(shape(*o) for o in hbm + outs) + (shape((early, 2, width, units), bf16),),
        scratch_shapes=[
            pltpu.SemaphoreType.DMA((nsem,)),
            pltpu.SemaphoreType.DMA((nsem,)),
            pltpu.VMEM((3, hn, width + RANK, half), bf16),
            pltpu.VMEM((hn, width + RANK, half), bf16),
            pltpu.SemaphoreType.DMA((6,)),
            pltpu.SemaphoreType.DMA((5, 2)),
            pltpu.VMEM((3, rows, half), bf16),
            pltpu.VMEM((rows, half), bf16),
            pltpu.VMEM((rows, units), bf16),
            pltpu.VMEM((early, rows, units), bf16),
            pltpu.VMEM((3, hn, RANK, half), bf16),
            pltpu.VMEM((hn, RANK, half), bf16),
            pltpu.VMEM((tn, 2, EXTRA, units), bf16),
            pltpu.VMEM((3, n, width), bf16),
            pltpu.VMEM((n, width + RANK), bf16),
            pltpu.VMEM((width, n), f32),
            pltpu.VMEM((width, n), f32),
            pltpu.VMEM((n, width), f32),
            tail_shape(length, width),
            pltpu.SemaphoreType.DMA((2,)),
        ],
        compiler_params=params(collective_id=3, has_side_effects=True),
        name="attention",
    )(wq, wo, wu, wd, bq, bp, bu, bd, ub, index, first, out, x, vectors, up)


def gelu_both(v, g):
    c, a = 0.7978845608028654, 0.044715
    sq = v * v
    t = jnp.tanh(v * (c + (c * a) * sq))
    half = 0.5 * (1.0 + t)
    slope = half + (0.5 * v) * ((1.0 - t * t) * (c + (3.0 * c * a) * sq))
    return v * half, g * slope


def mlp_half(ln_ref, g_ref, wu_ref, wd_ref, act_ref, gb_ref, out_acc, g_acc, rows, first, between):
    before = nn(ln_ref[rows, :], wu_ref[...])
    g_act = nn(g_ref[rows, :], wd_ref[...])
    act, gb = gelu_both(before, g_act)
    act, gb = act.astype(bf16), gb.astype(bf16)
    act_ref[rows, :] = act
    gb_ref[rows, :] = gb
    between()
    o, g = nt(act, wd_ref[...]), nt(gb, wu_ref[...])

    @pl.when(first)
    def _():
        out_acc[rows, :] = o
        g_acc[rows, :] = g

    @pl.when(jnp.logical_not(first))
    def _():
        out_acc[rows, :] += o
        g_acc[rows, :] += g


def mlp_kernel(
    sizes,
    length,
    plan,
    ln_ref,
    cot_ref,
    hidden_ref,
    early,
    zw,
    ax,
    index,
    up_bank,
    down_bank,
    vectors,
    y_ref,
    gh_ref,
    g_up_in,
    g_down_out,
    g_units,
    late,
    send,
    recv,
    w_buf,
    w_sems,
    g_buf,
    tail,
    gx,
    act,
    gb,
    out_acc,
    g_acc,
    sem,
    own_buf,
):
    i = pl.program_id(0)
    fn, hn, tn = sizes
    f, h, z = lax.axis_index("fsdp"), lax.axis_index("heads"), lax.axis_index("tensor")
    n, width = hidden_ref.shape
    number = index[(f * hn + h) * tn + z]
    gain, dbias = vectors.at[2:3], vectors.at[4:5]
    main = slice(0, width)
    s, half = i // 2, lax.rem(i, 2)
    comm = Comm(send, recv)
    done = early.shape[0]
    blocks = {b: Block(comm, sizes, zw, late.at[b - done], b, own_buf.at[b - done]) for b in range(done, tn)}

    def loads(b):
        slot = b % 2
        src = early.at[b] if b < done else late.at[b - done]
        return [
            pltpu.make_async_copy(src, w_buf.at[slot, :, pl.ds(0, width)], w_sems.at[slot, 0]),
            pltpu.make_async_copy(
                ax.at[:, lax.rem(z + b, tn)], w_buf.at[slot, :, pl.ds(width, EXTRA)], w_sems.at[slot, 1]
            ),
        ]

    @pl.when(i == 0)
    def _():
        c = Tokens(cot_ref, g_buf, tail, sem)
        c.start()
        for b in range(done):
            for w in loads(b):
                w.start()
        enter(sizes, f, h, z)
        if done in blocks:
            blocks[done].begin()
        c.wait()

        def body(rows, start):
            gx[rows, main] = g_buf[rows, :].astype(bf16)

        by_rows(n, 32, body)
        gx[:, width : width + RANK] = nt(gx[:, main], down_bank[number]).astype(bf16)
        gx[:, width + RANK :] = jnp.zeros((n, EXTRA - RANK), bf16)

    def events(steps):
        for at, what in steps:

            @pl.when(i == at)
            def _():
                for b, name in what:
                    if name == "load":
                        if b < tn:
                            if b in blocks:
                                blocks[b].arrive()
                            for w in loads(b):
                                w.start()
                    elif b in blocks:
                        getattr(blocks[b], name)()

    events(plan[0])

    for b in range(tn):

        @pl.when(i == 2 * b)
        def _():
            for w in loads(b):
                w.wait()

    slot = lax.rem(s, 2)
    rows = pl.ds(pl.multiple_of(half * (n // 2), n // 2), n // 2)
    mlp_half(ln_ref, gx, w_buf.at[slot, 0], w_buf.at[slot, 1], act, gb, out_acc, g_acc, rows, s == 0, lambda: events(plan[1]))

    @pl.when(half == 1)
    def _():
        g_units[0, s] = tn_(ln_ref[:, width : width + RANK], gb[...]).astype(bf16)
        g_units[1, s] = tn_(gx[:, width : width + RANK], act[...]).astype(bf16)

    @pl.when(i == pl.num_programs(0) - 1)
    def _():
        down_mid = out_acc[:, width : width + RANK].astype(bf16)
        g_up_mid = g_acc[:, width : width + RANK].astype(bf16)
        g_up_in[...] = tn_(g_up_mid, ln_ref[:, main]).astype(bf16)
        g_down_out[...] = tn_(down_mid, gx[:, main]).astype(bf16)
        out_acc[:, main] += nn(down_mid, down_bank[number])
        g_acc[:, main] += nn(g_up_mid, up_bank[number])

        def body(rows, start):
            v = hidden_ref[rows, :]
            out_acc[rows, main] += v + dbias[...]
            gh_ref[rows, :] = g_buf[rows, :] + real(
                norm_back(g_acc[rows, main], v, gain[...], width), start, length
            )

        by_rows(n, 32, body)
        c = Tokens(y_ref, out_acc, tail, sem, out=True)
        c.start()
        for b in blocks.values():
            b.drain()
        c.wait()


def mlp(sizes, ln, cot, hidden, early, zw, ax, index, up, down, vectors):
    fn, hn, tn = sizes
    n, width = hidden.shape
    depth = ln.shape[1]
    done, _, _, units = early.shape
    length = cot.shape[0]
    late = max(tn - done, 1)
    plan = (
        (
            (2, ((2, "forward"), (3, "begin"))),
            (3, ((2, "exchange"),)),
            (6, ((3, "load"),)),
        ),
        (
            (3, ((2, "load"),)),
            (4, ((3, "forward"),)),
            (5, ((3, "exchange"),)),
        ),
    )
    any_ = pl.BlockSpec(memory_space=pl.ANY)
    one = lambda s: pl.BlockSpec(s, lambda t: (0,) * len(s), pipeline_mode=pl.Buffered(1))
    shape = jax.ShapeDtypeStruct
    nsem = late * block_sems(fn)
    return pl.pallas_call(
        functools.partial(mlp_kernel, sizes, length, plan),
        grid=(2 * tn,),
        in_specs=[
            one((n, depth)),
            any_,
            one((n, width)),
            any_,
            any_,
            any_,
            pl.BlockSpec(memory_space=pltpu.SMEM),
            one(up.shape),
            one(down.shape),
            one(vectors.shape),
        ],
        out_specs=(
            any_,
            one((n, width)),
            one((RANK, width)),
            one((RANK, width)),
            one((2, tn, RANK, units)),
            any_,
        ),
        out_shape=(
            shape((length, 1, width), f32),
            shape((n, width), f32),
            shape((RANK, width), bf16),
            shape((RANK, width), bf16),
            shape((2, tn, RANK, units), bf16),
            shape((late, 2, width, units), bf16),
        ),
        scratch_shapes=[
            pltpu.SemaphoreType.DMA((nsem,)),
            pltpu.SemaphoreType.DMA((nsem,)),
            pltpu.VMEM((2, 2, depth, units), bf16),
            pltpu.SemaphoreType.DMA((2, 2)),
            pltpu.VMEM((n, width), f32),
            tail_shape(length, width),
            pltpu.VMEM((n, depth), bf16),
            pltpu.VMEM((n, units), bf16),
            pltpu.VMEM((n, units), bf16),
            pltpu.VMEM((n, depth), f32),
            pltpu.VMEM((n, depth), f32),
            pltpu.SemaphoreType.DMA((2,)),
            pltpu.VMEM((late,) + zw.shape[1:], bf16),
        ],
        compiler_params=params(collective_id=4, has_side_effects=True),
        name="mlp",
    )(ln, cot, hidden, early, zw, ax, index, up, down, vectors)


def branch_back_kernel(place, index, gh_ref, w_ref, out_bank, mixed_ref, mid_ref, g_up_in, g_down_out, gm_ref, grads, gx):
    n, width = gh_ref.shape
    half = w_ref.shape[-1]

    def body(rows, start):
        gx[rows, 0:width] = gh_ref[rows, :].astype(bf16)

    by_rows(n, 32, body)
    g_mid = nt(gx[:, 0:width], out_bank[index[place()]]).astype(bf16)
    gx[:, width:] = g_mid
    grads[...] = jnp.zeros_like(grads)
    grads[0:RANK, :] = tn_(mid_ref[...], gx[:, 0:width]).astype(bf16)
    grads[RANK : 2 * RANK, :] = g_up_in[...]
    grads[2 * RANK : 3 * RANK, :] = g_down_out[...]
    grads[3 * RANK : 4 * RANK, :] = tn_(g_mid, mixed_ref[...]).astype(bf16)
    for p in range(w_ref.shape[0]):
        gm_ref[:, p * half : (p + 1) * half] = nn(gx[...], w_ref[p]).astype(bf16)


def branch_back(rows, place, index, gh, w, out, mixed, mid, g_up_in, g_down_out):
    n, width = gh.shape
    return pl.pallas_call(
        functools.partial(branch_back_kernel, place),
        in_specs=[pl.BlockSpec(memory_space=pltpu.SMEM)] + [pl.BlockSpec(memory_space=pltpu.VMEM)] * 7,
        out_shape=(
            jax.ShapeDtypeStruct((n, width), bf16),
            jax.ShapeDtypeStruct((rows, width), bf16),
        ),
        scratch_shapes=[pltpu.VMEM((n, width + RANK), bf16)],
        compiler_params=params(),
        name="branch_back",
    )(index, gh, w, out, mixed, mid, g_up_in, g_down_out)


def add_by_adapter(pick, parts):
    width = parts.shape[-1]
    if parts.shape[-2] % 16:
        parts = parts.astype(f32)
    return nn(pick[...], parts.reshape(-1, width).astype(bf16))


def picks(adapters, count, rows):
    shape = (count * rows, adapters.shape[0] * rows)
    place = jnp.repeat(adapters * rows, rows) + jnp.tile(jnp.arange(rows), adapters.shape[0])
    return (lax.broadcasted_iota(jnp.int32, shape, 0) == place[None, :]).astype(bf16)


def line_copies(comm, tn, z, here, sems, own=None):
    up, down = sems

    def send(sem, block, to, src=None):
        return comm.copy(sem, here(block) if src is None else src, here(block), tensor=to)

    def begin():
        @pl.when(z < tn - 1)
        def _():
            send(up[0], z, z + 1, own).start()

        @pl.when(z > 0)
        def _():
            send(down[0], z, z - 1, own).start()

    def step(k, then):
        @pl.when(z - 1 - k >= 0)
        def _():
            b = z - 1 - k
            comm.copy(up[k], here(b), here(b), tensor=z - 1).wait_recv()
            if k + 1 < tn - 1:

                @pl.when(z < tn - 1)
                def _():
                    send(up[k + 1], b, z + 1).start()

            then(b)

        @pl.when(z + 1 + k < tn)
        def _():
            b = z + 1 + k
            comm.copy(down[k], here(b), here(b), tensor=z + 1).wait_recv()
            if k + 1 < tn - 1:

                @pl.when(z > 0)
                def _():
                    send(down[k + 1], b, z - 1).start()

            then(b)

    def drain():
        for k in range(tn - 1):

            @pl.when((z < tn - 1) & (z - k >= 0))
            def _():
                send(up[k], z, z + 1).wait_send()

            @pl.when((z > 0) & (z + k < tn))
            def _():
                send(down[k], z, z - 1).wait_send()

    return begin, step, drain


class Reduce:
    def __init__(self, sizes, count, comm, hot, local, a, out, ra, dense, b=None, out_b=None, rb=None, hot_b=None):
        fn, hn, tn = sizes
        f, h, z = lax.axis_index("fsdp"), lax.axis_index("heads"), lax.axis_index("tensor")
        self.fn, self.hn, self.tn, self.f, self.h, self.z = fn, hn, tn, f, h, z
        self.count, self.comm, self.hot, self.hot_b, self.local = count, comm, hot, hot_b, local
        self.a, self.out, self.ra, self.dense, self.b, self.out_b, self.rb = a, out, ra, dense, b, out_b, rb
        self.piece = ra.shape[1]
        self.s_first = [comm.new() for _ in range(fn - 1)]
        s_line = ([comm.new() for _ in range(tn - 1)], [comm.new() for _ in range(tn - 1)])
        self.s_core = [comm.new() for _ in range(tn)]
        self.s_last = comm.new()
        self.sent = []
        per = count // hn
        self.mine, self.theirs = pl.ds(h * per, per), pl.ds((1 - h) * per, per)

        def slot(o, r):
            start, size = (0, per) if r is None else r
            return out.at[o, pl.ds(h * per + start, size)]

        self.spread = Rows(comm, fn, f, slot, per, lambda: dense.at[self.mine], align=1)
        self.begin, self.line, self.drain_line = line_copies(
            comm, tn, z, lambda t: self.group(t, h), s_line
        )
        if b is not None:
            self.s_first_b = [comm.new() for _ in range(tn - 1)]
            self.s_core_b = comm.new()

            def slot_b(o, r):
                start, size = (0, tn) if r is None else r
                return rb.at[h, o, pl.ds(start, size)]

            self.spread_b = Rows(comm, fn, f, slot_b, tn, lambda: rb.at[h, f], align=1)

    def group(self, z, h):
        return self.ra.at[pl.ds((z * self.hn + h) * self.fn, self.fn)]

    def one(self, z, h, f):
        return self.ra.at[(z * self.hn + h) * self.fn + f]

    def rows(self, f):
        return self.a.at[pl.ds(pl.multiple_of(f * self.piece, 8), self.piece)]

    def send(self, make):
        make().start()
        self.sent.append(make)

    def own(self):
        copies = [pltpu.make_async_copy(self.rows(self.f), self.one(self.z, self.h, self.f), self.local.at[0])]
        if self.b is not None:
            copies.append(
                pltpu.make_async_copy(self.b.at[:, 0], self.rb.at[self.h, self.f, self.z], self.local.at[1])
            )
        return copies

    def start(self):
        f, h, z, comm = self.f, self.h, self.z, self.comm
        for m in range(1, self.fn):
            self.send(
                lambda m=m: comm.copy(
                    self.s_first[m - 1], self.rows(f ^ m), self.one(z, h, f), fsdp=f ^ m
                )
            )
        if self.b is not None:
            for d in range(1, self.tn):
                self.send(
                    lambda d=d: comm.copy(
                        self.s_first_b[d - 1],
                        self.b.at[:, d],
                        self.rb.at[h, f, z],
                        tensor=lax.rem(z + d, self.tn),
                    )
                )
        for c in self.own():
            c.start()

    def second(self):
        f, h, z, comm = self.f, self.h, self.z, self.comm
        for c in self.own():
            c.wait()
        for m in range(1, self.fn):
            b = self.one(z, h, f ^ m)
            comm.copy(self.s_first[m - 1], b, b, fsdp=f ^ m).wait_recv()
        self.begin()
        self.to_core(z).start()
        if self.b is not None:
            for d in range(1, self.tn):
                p = lax.rem(z + self.tn - d, self.tn)
                b = self.rb.at[h, f, p]
                comm.copy(self.s_first_b[d - 1], b, b, tensor=p).wait_recv()
            self.spread_b.begin()

    def to_core(self, block):
        b = self.group(block, self.h)
        return pltpu.make_async_remote_copy(
            src_ref=b,
            dst_ref=b,
            send_sem=self.comm.send.at[self.s_core[0] + block],
            recv_sem=self.comm.recv.at[self.s_core[0] + block],
            device_id={"heads": 1 - self.h},
            device_id_type=MESH,
        )

    def line_step(self, k):
        if k < self.tn - 1:
            self.line(k, lambda b: self.to_core(b).start())

    def forward_b(self):
        self.spread_b.forward_all()

    def exchange_b(self):
        self.spread_b.settle()
        b = self.rb.at[self.h]
        self.send(lambda: self.comm.copy(self.s_core_b, b, b, heads=1 - self.h))

    def fourth(self):
        h = self.h
        for k in range(self.tn):
            b = self.group(k, 1 - h)
            self.comm.copy(self.s_core[k], b, b, heads=1 - h).wait_recv()
        total = add_by_adapter(self.hot, self.ra[...])
        self.dense[...] = total.reshape(self.dense.shape).astype(bf16)
        self.spread.begin()
        self.last().start()

    def last(self):
        return pltpu.make_async_copy(
            self.dense.at[self.mine], self.out.at[self.f, self.mine], self.local.at[0]
        )

    def fifth(self):
        b = self.rb.at[1 - self.h]
        self.comm.copy(self.s_core_b, b, b, heads=1 - self.h).wait_recv()
        for k in range(2):
            total = add_by_adapter(self.hot_b, self.rb[:, :, :, k, :, :])
            self.out_b[k][...] = total.reshape(self.out_b[k].shape)

    def sixth(self):
        self.spread.forward_all()

    def seventh(self):
        self.last().wait()
        self.spread.settle()
        b = self.out.at[:, self.mine]
        self.send(lambda: self.comm.copy(self.s_last, b, b, heads=1 - self.h))

    def finish(self):
        h = self.h
        b = self.out.at[:, self.theirs]
        self.comm.copy(self.s_last, b, b, heads=1 - h).wait_recv()
        for make in self.sent:
            make().wait_send()
        self.drain_line()
        self.spread.drain()
        if self.b is not None:
            self.spread_b.drain()
        for k in range(self.tn):
            self.to_core(k).wait_send()


def reduce_sems(sizes, both):
    fn, hn, tn = sizes
    nb = bits_of(fn)
    tree = nb + 2 * (fn - 1 - nb)
    n = fn - 1 + 2 * (tn - 1) + tn + 1 + tree
    return n + (tn - 1 + 1 + tree if both else 0)


def enter_reduce(sizes, f, h, z):
    fn, hn, tn = sizes
    barrier = pltpu.get_barrier_semaphore()
    for m in range(1, fn):
        pl.semaphore_signal(barrier, 1, device_id={"fsdp": f ^ m}, device_id_type=MESH)
    pl.semaphore_signal(barrier, 1, device_id={"heads": 1 - h}, device_id_type=MESH)
    for d in range(1, tn):
        pl.semaphore_signal(barrier, 1, device_id={"tensor": lax.rem(z + d, tn)}, device_id_type=MESH)
    pl.semaphore_wait(barrier, fn - 1 + 1 + tn - 1)


def piece_rows(rows, fn):
    return -(-rows // (8 * fn)) * 8


def reduce_shapes(sizes, count, width, piece, units, both):
    fn, hn, tn = sizes
    n = fn * hn * tn
    shapes = [
        pltpu.SemaphoreType.DMA((reduce_sems(sizes, both),)),
        pltpu.SemaphoreType.DMA((reduce_sems(sizes, both),)),
        pltpu.SemaphoreType.DMA((2,)),
        pltpu.VMEM((n, piece, width), bf16),
        pltpu.VMEM((count, piece, width), bf16),
    ]
    if both:
        shapes.append(pltpu.VMEM((hn, fn, tn, 2, RANK, units), bf16))
    return shapes


def attend_back_kernel(
    sizes, length, count, plan, hot, hot_b, q_ref, k_ref, v_ref, do_ref, log_ref, a, b, out_ref, sums, sums_u, sums_d, send, recv, local, ra, dense, rb, kt_ref, dq_ref, dk_ref, dv_ref
):
    head = pl.program_id(0)
    job = Reduce(sizes, count, Comm(send, recv), hot, local, a, sums, ra, dense, b, (sums_u, sums_d), rb, hot_b)

    @pl.when(head == 0)
    def _():
        enter_reduce(sizes, job.f, job.h, job.z)
        job.start()
        to_rows(kt_ref, k_ref.at[0])

        def clear(at):
            for r in (dk_ref, dv_ref):
                r[:, at] = jnp.zeros((r.shape[0], LANES), f32)

        columns(dk_ref.shape[1], clear)

    for at, what in plan:

        @pl.when(head == at)
        def _():
            for name, *more in what:
                getattr(job, name)(*more)

    attend_back_head(
        length, head, q_ref.at[0], k_ref.at[0], v_ref.at[0], do_ref, log_ref, kt_ref, dq_ref, dk_ref, dv_ref
    )

    @pl.when(head == pl.num_programs(0) - 1)
    def _():
        to_lanes(out_ref.at[0], dq_ref)

        def cast(at):
            out_ref[1, :, at] = dk_ref[:, at].astype(bf16)
            out_ref[2, :, at] = dv_ref[:, at].astype(bf16)

        columns(dk_ref.shape[1], cast)
        job.finish()


def attend_back(sizes, length, count, hot, hot_b, qkv, do, log, a, b):
    fn, hn, tn = sizes
    _, n, width = qkv.shape
    heads = width // HEAD_DIM
    units = b.shape[-1]
    piece = a.shape[0] // fn
    plan = (
        (2, (("second",),)),
        (5, (("line_step", 0),)),
        (7, (("line_step", 1), ("forward_b",))),
        (9, (("line_step", 2), ("exchange_b",))),
        (11, (("fourth",),)),
        (12, (("fifth",),)),
        (13, (("sixth",),)),
        (15, (("seventh",),)),
    )
    any_ = pl.BlockSpec(memory_space=pl.ANY)
    one = lambda j: pl.BlockSpec((1, n, width), lambda h: (j, 0, 0), pipeline_mode=pl.Buffered(1))
    return pl.pallas_call(
        functools.partial(attend_back_kernel, sizes, length, count, plan),
        grid=(heads,),
        in_specs=[
            whole(hot.shape),
            whole(hot_b.shape),
            one(0),
            one(1),
            one(2),
            whole((n, width)),
            whole((heads, n)),
            any_,
            any_,
        ],
        out_specs=(whole((3, n, width)), any_) + (whole((count, RANK, units)),) * 2,
        out_shape=(
            jax.ShapeDtypeStruct((3, n, width), bf16),
            jax.ShapeDtypeStruct((fn, count, piece, width), bf16),
        )
        + (jax.ShapeDtypeStruct((count, RANK, units), f32),) * 2,
        scratch_shapes=reduce_shapes(sizes, count, width, piece, units, True)
        + [pltpu.VMEM((width, n), f32)] * 2
        + [pltpu.VMEM((n, width), f32)] * 2,
        compiler_params=params(collective_id=1, has_side_effects=True),
        name="attend_back",
    )(hot, hot_b, qkv, qkv, qkv, do, log, a, b)


def project_back_kernel(
    sizes,
    count,
    hot,
    index,
    before,
    g_ref,
    w_any,
    first_ref,
    mid_ref,
    ln_ref,
    gh_any,
    x_ref,
    vectors,
    gi_ref,
    sums,
    a,
    g_proj_out,
    g_up_in,
    g_down_out,
    g_proj_in,
    send,
    recv,
    local,
    ra,
    dense,
    w_buf,
    gh_buf,
    w_sems,
    x_buf,
    tail,
    acc,
    grads,
    g_mid,
    sem,
    before_buf,
):
    i = pl.program_id(0)
    length = x_ref.shape[0]
    n, width = ln_ref.shape
    half = w_buf.shape[-1]
    gain = vectors.at[0:1]
    parts = w_buf.shape[1]
    load = Tokens(x_ref, x_buf, tail, sem)
    job = Reduce(sizes, count, Comm(send, recv), hot, local, a, sums, ra, dense)
    number = index[(job.f * job.hn + job.h) * job.tn + job.z]

    def load_w(j):
        return pltpu.make_async_copy(w_any.at[j], w_buf.at[j], w_sems.at[j])

    load_gh = pltpu.make_async_copy(gh_any, gh_buf, w_sems.at[3])
    load_before = pltpu.make_async_copy(before, before_buf, w_sems.at[5])
    save = pltpu.make_async_copy(grads, a, w_sems.at[4])

    @pl.when(i == 0)
    def _():
        for j in range(3):
            load_w(j).start()
        load.start()
        load_gh.start()
        load_before.start()
        enter_reduce(sizes, job.f, job.h, job.z)
        if grads.shape[0] > 6 * RANK:
            grads[6 * RANK :, :] = jnp.zeros((grads.shape[0] - 6 * RANK, width), bf16)
        for j in range(3):
            load_w(j).wait()

        def small(j, _):
            m = sum(
                nt(g_ref[j, :, p * half : (p + 1) * half], w_buf[j, p, pl.ds(width, RANK), :])
                for p in range(parts)
            ).astype(bf16)
            g_mid[j] = m
            at = pl.ds(pl.multiple_of((3 + j) * RANK, RANK), RANK)
            grads[at, :] = tn_(mid_ref[j], g_ref[j]).astype(bf16)
            return 0

        lax.fori_loop(0, 3, small, 0)
        mids = jnp.concatenate([g_mid[j].astype(f32).T for j in range(3)]).astype(bf16)
        grads[0 : 3 * RANK, :] = nn(mids, ln_ref[...]).astype(bf16)
        save.start()
        save.wait()
        job.start()

    @pl.when(i == 2)
    def _():
        job.second()

    @pl.when(i == 3)
    def _():
        job.line_step(0)

    @pl.when((i > 0) & (i < 4))
    def _():
        j = i - 1
        r = nn(g_mid[j], first_ref[j, number])
        for p in range(parts):
            r = r + nt(g_ref[j, :, p * half : (p + 1) * half], w_buf[j, p, pl.ds(0, width), :])

        @pl.when(i == 1)
        def _():
            acc[...] = r

        @pl.when(i > 1)
        def _():
            acc[...] += r

    @pl.when(i == 4)
    def _():
        job.line_step(1)
        load.wait()
        load_gh.wait()

        def body(rows, start):
            v = x_buf[rows, :]
            acc[rows, :] = gh_buf[rows, :] + norm_back(acc[rows, :], v, gain[...], width)

        by_rows(n, 32, body)
        c = Tokens(gi_ref, acc, tail, sem, out=True)
        c.start()
        for k in range(2, sizes[2] - 1):
            job.line_step(k)
        job.fourth()
        load_before.wait()
        piece = before_buf.shape[2]

        def rows_of(k, r):
            k = k * RANK + r * 8
            return before_buf[k // piece, :, k % piece : k % piece + 8, :].astype(f32)

        for k, dst in enumerate((g_proj_out, g_up_in, g_down_out)):
            for r in range(2):
                dst[:, r * 8 : r * 8 + 8, :] = rows_of(k, r)

        for p in range(parts):

            @pl.when(job.h == p)
            def _():
                for r in range(2):
                    g_proj_in[:, r * 8 : r * 8 + 8, :] = rows_of(3, r)[:, :, p * half : (p + 1) * half]

        job.sixth()
        job.seventh()
        job.finish()
        c.wait()


def project_back(sizes, count, hot, index, before, g, w, first, mid, ln, gh, x, vectors):
    fn, hn, tn = sizes
    n, width = ln.shape
    half = w.shape[-1]
    length = x.shape[0]
    piece = piece_rows(6 * RANK, fn)
    any_ = pl.BlockSpec(memory_space=pl.ANY)
    one = lambda s: pl.BlockSpec(s, lambda t: (0,) * len(s), pipeline_mode=pl.Buffered(1))
    shape = jax.ShapeDtypeStruct
    return pl.pallas_call(
        functools.partial(project_back_kernel, sizes, count),
        grid=(5,),
        in_specs=[
            one(hot.shape),
            pl.BlockSpec(memory_space=pltpu.SMEM),
            any_,
            one(g.shape),
            any_,
            one(first.shape),
            one(mid.shape),
            one((n, width)),
            any_,
            any_,
            one(vectors.shape),
        ],
        out_specs=(any_, any_, any_) + (one((count, RANK, width)),) * 3 + (one((count, RANK, half)),),
        out_shape=(
            shape((length, 1, width), f32),
            shape((fn, count, piece, width), bf16),
            shape((fn * piece, width), bf16),
        )
        + (shape((count, RANK, width), f32),) * 3
        + (shape((count, RANK, half), f32),),
        scratch_shapes=reduce_shapes(sizes, count, width, piece, 0, False)
        + [
            pltpu.VMEM(w.shape, bf16),
            pltpu.VMEM((n, width), f32),
            pltpu.SemaphoreType.DMA((6,)),
            pltpu.VMEM((n, width), f32),
            tail_shape(length, width),
            pltpu.VMEM((n, width), f32),
            pltpu.VMEM((fn * piece, width), bf16),
            pltpu.VMEM(mid.shape, bf16),
            pltpu.SemaphoreType.DMA((2,)),
            pltpu.VMEM(before.shape, bf16),
        ],
        compiler_params=params(collective_id=2, has_side_effects=True),
        name="qkv_back",
    )(hot, index, before, g, w, first, mid, ln, gh, x, vectors)


def per_device(
    inputs,
    cotangent,
    image_adapter_index,
    first_norm_gain,
    first_norm_bias,
    second_norm_gain,
    second_norm_bias,
    query_key_value_weight,
    attention_output_weight,
    up_weight,
    down_weight,
    up_projection_bias,
    down_projection_bias,
    query_key_value_adapter_first,
    query_key_value_adapter_second,
    projection_adapter_first,
    projection_adapter_second,
    up_adapter_first,
    up_adapter_second,
    down_adapter_first,
    down_adapter_second,
):
    sizes = tuple(lax.axis_size(a) for a in ("fsdp", "heads", "tensor"))
    fn, hn, tn = sizes
    f, h, z = (lax.axis_index(a) for a in ("fsdp", "heads", "tensor"))
    images, length, width = inputs.shape
    assert images == 1 and hn == 2
    count = query_key_value_adapter_first.shape[1]
    units = up_weight.shape[-1]
    x, cot = jnp.swapaxes(inputs, 0, 1), jnp.swapaxes(cotangent, 0, 1)
    vectors = jnp.concatenate(
        [
            first_norm_gain,
            first_norm_bias,
            second_norm_gain,
            second_norm_bias,
            down_projection_bias.astype(f32),
        ]
    ).reshape(5, width)
    index = image_adapter_index
    qkv_in = jnp.swapaxes(query_key_value_adapter_first, 2, 3)
    u_in = jnp.swapaxes(up_adapter_first, 1, 2)
    wq, wo, zw, ax, ln1, qkv, qkv_mid, mixed, log, hidden, ln2, proj_mid, early = attention(
        sizes,
        jnp.swapaxes(query_key_value_weight, 0, 1),
        attention_output_weight,
        up_weight,
        down_weight,
        query_key_value_adapter_second,
        jnp.swapaxes(projection_adapter_first, 1, 2),
        up_adapter_second,
        down_adapter_first,
        jnp.pad(up_projection_bias[None], ((0, EXTRA - RANK - 1), (0, 0))),
        index,
        qkv_in,
        projection_adapter_second,
        x,
        vectors,
        u_in,
    )
    y, g_hidden, g_up_in, g_down_out, g_units, _ = mlp(
        sizes, ln2, cot, hidden, early, zw, ax, index, u_in, down_adapter_second, vectors
    )
    g_mixed, grads = branch_back(
        piece_rows(4 * RANK, fn) * fn,
        lambda: (lax.axis_index("fsdp") * hn + lax.axis_index("heads")) * tn + lax.axis_index("tensor"),
        index,
        g_hidden,
        wo,
        projection_adapter_second,
        mixed,
        proj_mid,
        g_up_in,
        g_down_out,
    )
    by_place = image_adapter_index.reshape(fn, hn, tn)
    order = jnp.transpose(by_place, (2, 1, 0)).reshape(-1)
    order_b = jnp.transpose(by_place, (1, 0, 2)).reshape(-1)
    pick = picks(order, count, piece_rows(4 * RANK, fn))
    pick_b = picks(order_b, count, RANK)
    g_qkv, sums, g_up_out, g_down_in = attend_back(
        sizes, length, count, pick, pick_b, qkv, g_mixed, log, grads, g_units
    )
    g_x, last, _, g_proj_out, g_up_in, g_down_out, g_proj_in = project_back(
        sizes,
        count,
        picks(order, count, piece_rows(6 * RANK, fn)),
        index,
        sums,
        g_qkv,
        wq,
        qkv_in,
        qkv_mid,
        ln1,
        g_hidden,
        x,
        vectors,
    )
    last = jnp.moveaxis(last, 0, 1).reshape(count, -1, width)
    last = jnp.moveaxis(last[:, : 6 * RANK].reshape(count, 6, RANK, width), 0, 1).astype(f32)
    half = width // hn
    return (
        jnp.swapaxes(y, 0, 1),
        jnp.swapaxes(g_x, 0, 1),
        jnp.swapaxes(last[:3], 2, 3),
        lax.dynamic_slice_in_dim(last[3:], h * half, half, axis=-1),
        jnp.swapaxes(g_proj_in, 1, 2),
        g_proj_out,
        jnp.swapaxes(g_up_in, 1, 2),
        g_up_out,
        g_down_in,
        g_down_out,
    )


def solution(mesh):
    in_specs = (
        P(("fsdp", "heads", "tensor"), None, None),
        P(("fsdp", "heads", "tensor"), None, None),
        P(),
        P(),
        P(),
        P(),
        P(),
        P("fsdp", None, "heads"),
        P("fsdp", "heads"),
        P("fsdp", "tensor"),
        P("fsdp", "tensor"),
        P("tensor"),
        P(),
        P(),
        P(None, None, None, "heads"),
        P(None, "heads", None),
        P(),
        P(),
        P(None, None, "tensor"),
        P(None, None, "tensor"),
        P(),
    )
    out_specs = (
        P(("fsdp", "heads", "tensor"), None, None),
        P(("fsdp", "heads", "tensor"), None, None),
        P(),
        P(None, None, None, "heads"),
        P(None, "heads", None),
        P(),
        P(),
        P(None, None, "tensor"),
        P(None, None, "tensor"),
        P(),
    )
    return jax.shard_map(
        per_device, mesh=mesh, in_specs=in_specs, out_specs=out_specs, check_vma=False
    )
```

profile of v0, /device:TPU:0, one launch (start us, length us, event | category | flops | bytes accessed | tf_op | source)
XLA Modules:
  0.0 332.5 jit_solution(7079076505704447480)
XLA Ops:
  0.7 0.7 constant_dynamic-update-slice_fusion.3
  1.4 0.7 constant_dynamic-update-slice_fusion.2
  2.1 0.7 constant_dynamic-update-slice_fusion.1
  2.8 0.7 constant_dynamic-update-slice_fusion
  3.5 0.7 convert_dynamic-update-slice_fusion
  6.1 114.5 %attention.1 = (bf16[3,2,1168,576]{3,2,1,0:T(8,128)(2,1)}, bf16[2,1168,576]{2,1,0:T(8,128)(2,1)}, bf16[4,288,1076]{2,1,0:T(8,128)(2,1)}, bf16[2,4,32,1076]{3,2,1...) custom-call(bf16[3,288,576]{2,1,0:T(8,128)(2,1)} %bitcast.30, ...), custom_call_target="tpu_custom_call" | custom-call | tf_op jit(solution)/shard_map/attention/pallas_call | solution.py:689
  120.6 86.7 %mlp.1 = (f32[729,1,1152]{2,1,0:T(1,128)}, f32[736,1152]{1,0:T(8,128)}, bf16[16,1152]{1,0:T(8,128)(2,1)}, bf16[16,1152]{1,0:T(8,128)(2,1)}, bf16[2,4,16,1076]{3,...) custom-call(bf16[736,1184]{1,0:T(8,128)(2,1)} %get-tuple-element.40.ln_ref, f32[729,1,1152]{2,1,0:T(1,128)} %bitcast.27, ...), custom_call_target="tpu_custom_call" | custom-call | tf_op jit(solution)/shard_map/mlp/pallas_call | solution.py:910
  207.3 9.2 %branch_back.1 = (bf16[736,1152]{1,0:T(8,128)(2,1)}, bf16[64,1152]{1,0:T(8,128)(2,1)}) custom-call(s32[32]{0:T(128)} %index.7, f32[736,1152]{1,0:T(8,128)} %get-tuple-element.47.gh_ref.gh_any, bf16[2,1168,576]{2,1,0:T(8,128)(2,1)} %get-tuple-element.48.w_ref, bf16[8,16,1152]{2,1,0:T(8,128)(2,1)} %out_bank.1, bf16[736,1152]{1,0:T(8,128)(2,1)} %get-tuple-element.49.mixed_ref, ...), custom_call_target="tpu_custom_call" | custom-call | tf_op jit(solution)/shard_map/branch_back/pallas_call | solution.py:982
  217.2 0.8 fusion.1
  218.0 48.9 %attend_back.1 = (bf16[3,736,1152]{2,1,0:T(8,128)(2,1)}, bf16[4,8,16,1152]{3,2,1,0:T(8,128)(2,1)}, f32[8,16,1076]{2,1,0:T(8,128)}, f32[8,16,1076]{2,1,0:T(8,128)}) custom-call(bf16[128,512]{1,0:T(8,128)(2,1)} %get-tuple-element.84.hot, bf16[128,512]{1,0:T(8,128)(2,1)} %get-tuple-element.85.hot_b, bf16[3,736,1152]{2,1,0:T(8,128)(2,1)} %get-tuple-element.46.q_ref.k_ref.v_ref, ...), custom_call_target="tpu_custom_call" | custom-call | tf_op jit(solution)/shard_map/attend_back/pallas_call | solution.py:1319
  267.3 0.8 fusion.hot
  268.1 49.7 %qkv_back.1 = (f32[729,1,1152]{2,1,0:T(1,128)}, bf16[4,8,24,1152]{3,2,1,0:T(8,128)(2,1)}, bf16[96,1152]{1,0:T(8,128)(2,1)}, f32[8,16,1152]{2,1,0:T(8,128)}, f32[...) custom-call(bf16[192,768]{1,0:T(8,128)(2,1)} %fusion.hot, s32[32]{0:T(128)} %index.7, ...), custom_call_target="tpu_custom_call" | custom-call | tf_op jit(solution)/shard_map/qkv_back/pallas_call | solution.py:1503
  317.8 1.7 convert_bitcast_fusion
  320.4 1.0 copy.39
  321.4 1.3 copy.38
  322.8 1.7 copy.53
  324.5 1.4 copy-done.1
  326.0 1.7 copy.54
  327.7 0.7 copy.55
  328.4 0.8 copy.56
  329.2 0.8 copy.57
  330.1 0.8 copy.58
  330.9 0.8 copy.59
  331.7 0.8 copy.60
  (39 shorter events, 3.9 us)
Async XLA Ops:
  207.3 9.2 %copy-start.8 = (s32[32]{0:T(128)S(1)}, s32[32]{0:T(128)}, u32[]{:S(2)}) copy-start(s32[32]{0:T(128)} %index.7) | copy-start | bytes 388
  320.1 2.7 copy-start
  322.8 3.2 copy-start.1
  325.9 1.8 copy-start.7
  325.9 2.5 copy-start.6
  326.0 3.3 copy-start.5
  326.0 4.1 %copy-start.3 = (f32[8,16,1076]{2,1,0:T(8,128)S(1)}, f32[8,16,1076]{2,1,0:T(8,128)}, u32[]{:S(2)}) copy-start(f32[8,16,1076]{2,1,0:T(8,128)} %get-tuple-element.103) | copy-start | bytes 1652740
  327.7 3.2 copy-start.2
  327.7 4.0 %copy-start.4 = (f32[8,16,1152]{2,1,0:T(8,128)S(1)}, f32[8,16,1152]{2,1,0:T(8,128)}, u32[]{:S(2)}) copy-start(f32[8,16,1152]{2,1,0:T(8,128)} %get-tuple-element.105) | copy-start | bytes 1769476
where the time goes:
time: 333 us
  Pallas kernels  309 us (93%)
  local copies, waits for them, and re-layouts  18.6 us (6%)
  other arithmetic  4.17 us (1%)
    pallas_call x1, Pallas kernels, attention(): pl.pallas_call(functools.partial(attention_kernel, sizes), grid=(6 + head...  114 us
    pallas_call x1, Pallas kernels, mlp(): pl.pallas_call(functools.partial(mlp_kernel, sizes, length, plan), grid=(...  86.7 us
    pallas_call x1, Pallas kernels, project_back(): pl.pallas_call(functools.partial(project_back_kernel, sizes, count), grid...  49.7 us
    pallas_call x1, Pallas kernels, attend_back(): pl.pallas_call(functools.partial(attend_back_kernel, sizes, length, count...  48.9 us
    unnamed x32, local copies, waits for them, and re-layouts  14.9 us
    pallas_call x1, Pallas kernels, branch_back(): pl.pallas_call(functools.partial(branch_back_kernel, place), in_specs=[pl...  9.22 us

commit v1 on v0

--- a/solution.py
+++ b/solution.py
@@ -241,6 +241,7 @@
                 for b in order[last + 1 :]:
                     self.later[p, m, b] = comm.new()
         self.sent = []
+        self.first_done = False
 
     def part(self, origin, p):
         start, size, _ = self.parts[p]
@@ -265,7 +266,7 @@
         return self.comm.copy(self.later[p, src, b], where, where, fsdp=self.f ^ (1 << b))
 
     def forward(self, m):
-        if m & (m - 1) == 0:
+        if m & (m - 1) == 0 and not self.first_done:
             b = bits_of(m)
             where = self.slot(self.f ^ m, None)
             self.comm.copy(self.first[b], where, where, fsdp=self.f ^ m).wait_recv()
@@ -283,6 +284,12 @@
 
     def masks(self):
         return sorted(range(1, self.fn), key=lambda m: (bin(m).count("1"), m))
+
+    def finish_first(self):
+        for b in range(self.nb):
+            where = self.slot(self.f ^ (1 << b), None)
+            self.comm.copy(self.first[b], where, where, fsdp=self.f ^ (1 << b)).wait_recv()
+        self.drain()
 
     def leaf(self, m):
         return not any(key[1] == m for key in self.later)
@@ -494,8 +501,9 @@
     small = [comm.new() for _ in range(tn - 1)]
     blocks = [
         Block(comm, sizes, zw, got.at[b], b, own_b.at[b], own_z if b == 0 else None)
-        for b in range(got.shape[0])
+        for b in range(own_b.shape[0])
     ]
+    nxt = [Block(comm, sizes, zw, got.at[b], b, own_z) for b in range(len(blocks), min(len(blocks) + 2, tn))]
     begin_z, step_z, drain_z = line_copies(comm, tn, z, lambda t: zw.at[t], line, own_z)
     mine_z = [Bounce(w, own_z, zw.at[z], own_sems.at[4, 0]) for w in (wu, wd)]
     mine_a = lambda: pltpu.make_async_copy(a2.at[z], ax.at[:, z], own_sems.at[4, 1])
@@ -551,8 +559,8 @@
         qs[0].job.forward_all()
         qs[2].job.begin()
         qs[1].job.forward_all()
+        step_z(0, lambda t: None)
         qs[0].exchange()
-        step_z(0, lambda t: None)
         qs[0].arrive()
         load_q(0).start()
 
@@ -561,14 +569,14 @@
         qs[2].job.forward_all()
         o.job.begin()
         qs[1].exchange()
-        if tn > 2:
-            step_z(1, lambda t: None)
         qs[1].arrive()
         load_q(1).start()
         qs[2].exchange()
 
     @pl.when(i == 3)
     def _():
+        if tn > 2:
+            step_z(1, lambda t: None)
         qs[2].arrive()
         load_q(2).start()
 
@@ -592,26 +600,30 @@
         save_qkv().start()
         o.job.forward_all()
         blocks[0].begin()
+        to_rows(vt_ref, qkv_ref.at[2])
+
+    @pl.when(i == 8)
+    def _():
+        o.exchange()
+
+    @pl.when(i == 11)
+    def _():
+        o.arrive()
+        load_o().start()
+
+    @pl.when(i == 9)
+    def _():
         for k in range(2, tn - 1):
             step_z(k, lambda t: None)
-        for b in blocks[1:]:
-            b.begin()
-        to_rows(vt_ref, qkv_ref.at[2])
-
-    @pl.when(i == 8)
-    def _():
-        o.exchange()
-
-    @pl.when(i == 11)
-    def _():
-        o.arrive()
-        load_o().start()
-
-    for b in range(got.shape[0]):
-
-        @pl.when(i == 16 + 3 * b)
-        def _():
-            blocks[b].forward()
+        for b in nxt[:1]:
+            b.job.begin()
+
+    @pl.when(i == 14)
+    def _():
+        for b in blocks:
+            b.forward()
+        for b in nxt[1:]:
+            b.job.begin()
 
     @pl.when((i >= 4) & (i < 4 + heads))
     def _():
@@ -619,7 +631,6 @@
 
     @pl.when(i == 4 + heads)
     def _():
-        blocks[0].exchange()
         to_lanes(mixed_ref, sum_ref)
         load_o().wait()
         br = sum(nt(mixed_ref[:, p * half : (p + 1) * half], wo_buf[p]) for p in range(hn))
@@ -629,9 +640,6 @@
 
     @pl.when(i == 5 + heads)
     def _():
-        for b in blocks[1:]:
-            b.exchange()
-
         def body(rows, start):
             v = real(x_buf[rows, :] + hidden_ref[rows, :], start, length)
             hidden_ref[rows, :] = v
@@ -643,6 +651,8 @@
         lane = lax.broadcasted_iota(jnp.int32, (n, EXTRA - RANK), 1)
         ln2_ref[:, width : width + RANK] = up_mid.astype(bf16)
         ln2_ref[:, width + RANK :] = (lane == 0).astype(bf16)
+        for b in blocks:
+            b.exchange()
         save_qkv().wait()
         mine_z[0].wait()
         mine_a().wait()
@@ -655,6 +665,8 @@
             b.arrive()
         for w in qs + [o] + blocks:
             w.drain()
+        for b in nxt:
+            b.job.finish_first()
 
 
 def attention(sizes, wq, wo, wu, wd, bq, bp, bu, bd, ub, index, first, out, x, vectors, up):
@@ -665,11 +677,11 @@
     length = x.shape[0]
     n = padded(length)
     heads = width // HEAD_DIM
-    early = min(2, tn)
+    early = 1
     any_ = pl.BlockSpec(memory_space=pl.ANY)
     one = lambda s: pl.BlockSpec(s, lambda i: (0,) * len(s), pipeline_mode=pl.Buffered(1))
     shape = jax.ShapeDtypeStruct
-    nsem = 4 * (tree_sems(fn) + 2) + 3 * (tn - 1) + early * block_sems(fn)
+    nsem = 4 * (tree_sems(fn) + 2) + 3 * (tn - 1) + (early + 2) * block_sems(fn)
     hbm = [
         ((3, hn, width + RANK, half), bf16),
         ((hn, width + RANK, half), bf16),
@@ -694,7 +706,7 @@
         + [pl.BlockSpec(memory_space=pltpu.SMEM)]
         + [one(first.shape), one(out.shape), any_, one(vectors.shape), one(up.shape)],
         out_specs=(any_,) * len(hbm) + tuple(one(s) for s, _ in outs) + (any_,),
-        out_shape=tuple(shape(*o) for o in hbm + outs) + (shape((early, 2, width, units), bf16),),
+        out_shape=tuple(shape(*o) for o in hbm + outs) + (shape((tn, 2, width, units), bf16),),
         scratch_shapes=[
             pltpu.SemaphoreType.DMA((nsem,)),
             pltpu.SemaphoreType.DMA((nsem,)),
@@ -755,6 +767,7 @@
 def mlp_kernel(
     sizes,
     length,
+    done,
     plan,
     ln_ref,
     cot_ref,
@@ -795,14 +808,15 @@
     main = slice(0, width)
     s, half = i // 2, lax.rem(i, 2)
     comm = Comm(send, recv)
-    done = early.shape[0]
-    blocks = {b: Block(comm, sizes, zw, late.at[b - done], b, own_buf.at[b - done]) for b in range(done, tn)}
+    blocks = {b: Block(comm, sizes, zw, late.at[b], b, own_buf.at[b - done]) for b in range(done, tn)}
+    resumed = [blocks[b] for b in range(done, min(done + 2, tn))]
+    for b in resumed:
+        b.job.first_done = True
 
     def loads(b):
         slot = b % 2
-        src = early.at[b] if b < done else late.at[b - done]
         return [
-            pltpu.make_async_copy(src, w_buf.at[slot, :, pl.ds(0, width)], w_sems.at[slot, 0]),
+            pltpu.make_async_copy(late.at[b], w_buf.at[slot, :, pl.ds(0, width)], w_sems.at[slot, 0]),
             pltpu.make_async_copy(
                 ax.at[:, lax.rem(z + b, tn)], w_buf.at[slot, :, pl.ds(width, EXTRA)], w_sems.at[slot, 1]
             ),
@@ -815,9 +829,13 @@
         for b in range(done):
             for w in loads(b):
                 w.start()
+        for b in resumed:
+            b.mine().start()
         enter(sizes, f, h, z)
-        if done in blocks:
-            blocks[done].begin()
+        for b in resumed:
+            b.forward()
+        for b in range(done + 2, tn):
+            blocks[b].begin()
         c.wait()
 
         def body(rows, start):
@@ -888,19 +906,21 @@
     fn, hn, tn = sizes
     n, width = hidden.shape
     depth = ln.shape[1]
-    done, _, _, units = early.shape
+    units = early.shape[-1]
+    done = 1
     length = cot.shape[0]
     late = max(tn - done, 1)
     plan = (
         (
-            (2, ((2, "forward"), (3, "begin"))),
-            (3, ((2, "exchange"),)),
-            (6, ((3, "load"),)),
-        ),
-        (
+            (2, ((2, "exchange"),)),
             (3, ((2, "load"),)),
             (4, ((3, "forward"),)),
             (5, ((3, "exchange"),)),
+        ),
+        (
+            (0, ((1, "exchange"),)),
+            (1, ((1, "load"),)),
+            (5, ((3, "load"),)),
         ),
     )
     any_ = pl.BlockSpec(memory_space=pl.ANY)
@@ -908,7 +928,7 @@
     shape = jax.ShapeDtypeStruct
     nsem = late * block_sems(fn)
     return pl.pallas_call(
-        functools.partial(mlp_kernel, sizes, length, plan),
+        functools.partial(mlp_kernel, sizes, length, done, plan),
         grid=(2 * tn,),
         in_specs=[
             one((n, depth)),
@@ -936,8 +956,9 @@
             shape((RANK, width), bf16),
             shape((RANK, width), bf16),
             shape((2, tn, RANK, units), bf16),
-            shape((late, 2, width, units), bf16),
+            shape(early.shape, bf16),
         ),
+        input_output_aliases={3: 6 - 1},
         scratch_shapes=[
             pltpu.SemaphoreType.DMA((nsem,)),
             pltpu.SemaphoreType.DMA((nsem,)),

time: 333 us -> 326 us (0.979)
  Pallas kernels: 309 us -> 302 us
    pallas_call x1, Pallas kernels: 86.7 us -> 79.6 us  [mlp(): pl.pallas_call(functools.partial(mlp_kernel, sizes, length, done, plan),...]
where the time goes in v1:
time: 326 us; the launch traced here: 325 us
  Pallas kernels  302 us (93%)
  local copies, waits for them, and re-layouts  18.6 us (6%)
  other arithmetic  4.17 us (1%)
    pallas_call x1, Pallas kernels, attention(): pl.pallas_call(functools.partial(attention_kernel, sizes), grid=(6 + head...  115 us
    pallas_call x1, Pallas kernels, mlp(): pl.pallas_call(functools.partial(mlp_kernel, sizes, length, done, plan),...  79.6 us
    pallas_call x1, Pallas kernels, project_back(): pl.pallas_call(functools.partial(project_back_kernel, sizes, count), grid...  49.4 us
    pallas_call x1, Pallas kernels, attend_back(): pl.pallas_call(functools.partial(attend_back_kernel, sizes, length, count...  48.4 us
    unnamed x32, local copies, waits for them, and re-layouts  14.9 us
    pallas_call x1, Pallas kernels, branch_back(): pl.pallas_call(functools.partial(branch_back_kernel, place), in_specs=[pl...  9.22 us

profile of v1, /device:TPU:0, one launch (start us, length us, event | category | flops | bytes accessed | tf_op | source)
XLA Modules:
  0.0 325.3 jit_solution(64519558749587103)
XLA Ops:
  0.7 0.7 constant_dynamic-update-slice_fusion.3
  1.4 0.7 constant_dynamic-update-slice_fusion.2
  2.1 0.7 constant_dynamic-update-slice_fusion.1
  2.8 0.7 constant_dynamic-update-slice_fusion
  3.5 0.7 convert_dynamic-update-slice_fusion
  6.1 115.1 %attention.1 = (bf16[3,2,1168,576]{3,2,1,0:T(8,128)(2,1)}, bf16[2,1168,576]{2,1,0:T(8,128)(2,1)}, bf16[4,288,1076]{2,1,0:T(8,128)(2,1)}, bf16[2,4,32,1076]{3,2,1...) custom-call(bf16[3,288,576]{2,1,0:T(8,128)(2,1)} %bitcast.30, ...), custom_call_target="tpu_custom_call" | custom-call | tf_op jit(solution)/shard_map/attention/pallas_call | solution.py:701
  121.2 79.6 %mlp.1 = (f32[729,1,1152]{2,1,0:T(1,128)}, f32[736,1152]{1,0:T(8,128)}, bf16[16,1152]{1,0:T(8,128)(2,1)}, bf16[16,1152]{1,0:T(8,128)(2,1)}, bf16[2,4,16,1076]{3,...) custom-call(bf16[736,1184]{1,0:T(8,128)(2,1)} %get-tuple-element.40.ln_ref, ...), custom_call_target="tpu_custom_call", output_to_operand_aliasing={{5}: (3, {})} | custom-call | tf_op jit(solution)/shard_map/mlp/pallas_call | solution.py:930
  200.8 9.2 %branch_back.1 = (bf16[736,1152]{1,0:T(8,128)(2,1)}, bf16[64,1152]{1,0:T(8,128)(2,1)}) custom-call(s32[32]{0:T(128)} %index.7, f32[736,1152]{1,0:T(8,128)} %get-tuple-element.47.gh_ref.gh_any, bf16[2,1168,576]{2,1,0:T(8,128)(2,1)} %get-tuple-element.48.w_ref, bf16[8,16,1152]{2,1,0:T(8,128)(2,1)} %out_bank.1, bf16[736,1152]{1,0:T(8,128)(2,1)} %get-tuple-element.49.mixed_ref, ...), custom_call_target="tpu_custom_call" | custom-call | tf_op jit(solution)/shard_map/branch_back/pallas_call | solution.py:1003
  210.7 0.8 fusion.1
  211.5 48.4 %attend_back.1 = (bf16[3,736,1152]{2,1,0:T(8,128)(2,1)}, bf16[4,8,16,1152]{3,2,1,0:T(8,128)(2,1)}, f32[8,16,1076]{2,1,0:T(8,128)}, f32[8,16,1076]{2,1,0:T(8,128)}) custom-call(bf16[128,512]{1,0:T(8,128)(2,1)} %get-tuple-element.84.hot, bf16[128,512]{1,0:T(8,128)(2,1)} %get-tuple-element.85.hot_b, bf16[3,736,1152]{2,1,0:T(8,128)(2,1)} %get-tuple-element.46.q_ref.k_ref.v_ref, ...), custom_call_target="tpu_custom_call" | custom-call | tf_op jit(solution)/shard_map/attend_back/pallas_call | solution.py:1340
  260.4 0.8 fusion.hot
  261.1 49.4 %qkv_back.1 = (f32[729,1,1152]{2,1,0:T(1,128)}, bf16[4,8,24,1152]{3,2,1,0:T(8,128)(2,1)}, bf16[96,1152]{1,0:T(8,128)(2,1)}, f32[8,16,1152]{2,1,0:T(8,128)}, f32[...) custom-call(bf16[192,768]{1,0:T(8,128)(2,1)} %fusion.hot, s32[32]{0:T(128)} %index.7, ...), custom_call_target="tpu_custom_call" | custom-call | tf_op jit(solution)/shard_map/qkv_back/pallas_call | solution.py:1524
  310.5 1.7 convert_bitcast_fusion
  313.1 1.0 copy.40
  314.2 1.3 copy.39
  315.5 1.7 copy.55
  317.3 1.4 copy-done.1
  318.7 1.7 copy.56
  320.4 0.7 copy.57
  321.2 0.8 copy.58
  322.0 0.8 copy.59
  322.8 0.8 copy.60
  323.6 0.8 copy.61
  324.4 0.8 copy.62
  (39 shorter events, 3.9 us)
Async XLA Ops:
  200.8 9.2 %copy-start.8 = (s32[32]{0:T(128)S(1)}, s32[32]{0:T(128)}, u32[]{:S(2)}) copy-start(s32[32]{0:T(128)} %index.7) | copy-start | bytes 388
  312.8 2.7 copy-start
  315.5 3.2 copy-start.1
  318.7 1.8 copy-start.7
  318.7 2.5 copy-start.6
  318.7 3.3 %copy-start.5 = (f32[8,16,1152]{2,1,0:T(8,128)S(1)}, f32[8,16,1152]{2,1,0:T(8,128)}, u32[]{:S(2)}) copy-start(f32[8,16,1152]{2,1,0:T(8,128)} %get-tuple-element.66) | copy-start | bytes 1769476
  318.7 4.1 %copy-start.3 = (f32[8,16,1076]{2,1,0:T(8,128)S(1)}, f32[8,16,1076]{2,1,0:T(8,128)}, u32[]{:S(2)}) copy-start(f32[8,16,1076]{2,1,0:T(8,128)} %get-tuple-element.103) | copy-start | bytes 1652740
  320.4 3.2 copy-start.2
  320.4 4.0 %copy-start.4 = (f32[8,16,1152]{2,1,0:T(8,128)S(1)}, f32[8,16,1152]{2,1,0:T(8,128)}, u32[]{:S(2)}) copy-start(f32[8,16,1152]{2,1,0:T(8,128)} %get-tuple-element.105) | copy-start | bytes 1769476

commit v2 on v1

--- a/solution.py
+++ b/solution.py
@@ -979,9 +979,13 @@
     )(ln, cot, hidden, early, zw, ax, index, up, down, vectors)
 
 
-def branch_back_kernel(place, index, gh_ref, w_ref, out_bank, mixed_ref, mid_ref, g_up_in, g_down_out, gm_ref, grads, gx):
+def branch_back_kernel(
+    place, index, gh_ref, w_ref, out_bank, mixed_ref, mid_ref, g_up_in, g_down_out, y_in, gm_ref, grads, y_out, gx, y_buf, sem
+):
     n, width = gh_ref.shape
     half = w_ref.shape[-1]
+    y = Bounce(y_in, y_buf, y_out, sem)
+    y.start()
 
     def body(rows, start):
         gx[rows, 0:width] = gh_ref[rows, :].astype(bf16)
@@ -996,21 +1000,31 @@
     grads[3 * RANK : 4 * RANK, :] = tn_(g_mid, mixed_ref[...]).astype(bf16)
     for p in range(w_ref.shape[0]):
         gm_ref[:, p * half : (p + 1) * half] = nn(gx[...], w_ref[p]).astype(bf16)
-
-
-def branch_back(rows, place, index, gh, w, out, mixed, mid, g_up_in, g_down_out):
+        if p == 0:
+            y.turn()
+    y.wait()
+
+
+def branch_back(rows, place, index, gh, w, out, mixed, mid, g_up_in, g_down_out, y):
     n, width = gh.shape
     return pl.pallas_call(
         functools.partial(branch_back_kernel, place),
-        in_specs=[pl.BlockSpec(memory_space=pltpu.SMEM)] + [pl.BlockSpec(memory_space=pltpu.VMEM)] * 7,
+        in_specs=[pl.BlockSpec(memory_space=pltpu.SMEM)] + [pl.BlockSpec(memory_space=pltpu.VMEM)] * 7
+        + [pl.BlockSpec(memory_space=pl.ANY)],
+        out_specs=(pl.BlockSpec(memory_space=pltpu.VMEM),) * 2 + (pl.BlockSpec(memory_space=pl.ANY),),
         out_shape=(
             jax.ShapeDtypeStruct((n, width), bf16),
             jax.ShapeDtypeStruct((rows, width), bf16),
+            jax.ShapeDtypeStruct(y.shape, f32),
         ),
-        scratch_shapes=[pltpu.VMEM((n, width + RANK), bf16)],
+        scratch_shapes=[
+            pltpu.VMEM((n, width + RANK), bf16),
+            pltpu.VMEM(y.shape, f32),
+            pltpu.SemaphoreType.DMA(()),
+        ],
         compiler_params=params(),
         name="branch_back",
-    )(index, gh, w, out, mixed, mid, g_up_in, g_down_out)
+    )(index, gh, w, out, mixed, mid, g_up_in, g_down_out, y)
 
 
 def add_by_adapter(pick, parts):
@@ -1100,7 +1114,7 @@
             start, size = (0, per) if r is None else r
             return out.at[o, pl.ds(h * per + start, size)]
 
-        self.spread = Rows(comm, fn, f, slot, per, lambda: dense.at[self.mine], align=1)
+        self.spread = Rows(comm, fn, f, slot, per, lambda: dense, align=1)
         self.begin, self.line, self.drain_line = line_copies(
             comm, tn, z, lambda t: self.group(t, h), s_line
         )
@@ -1200,14 +1214,16 @@
         for k in range(self.tn):
             b = self.group(k, 1 - h)
             self.comm.copy(self.s_core[k], b, b, heads=1 - h).wait_recv()
-        total = add_by_adapter(self.hot, self.ra[...])
+        rows = self.hot.shape[0] // self.hn
+        mine = self.hot.at[pl.ds(pl.multiple_of(self.h * rows, 16), rows)]
+        total = add_by_adapter(mine, self.ra[...])
         self.dense[...] = total.reshape(self.dense.shape).astype(bf16)
         self.spread.begin()
         self.last().start()
 
     def last(self):
         return pltpu.make_async_copy(
-            self.dense.at[self.mine], self.out.at[self.f, self.mine], self.local.at[0]
+            self.dense, self.out.at[self.f, self.mine], self.local.at[0]
         )
 
     def fifth(self):
@@ -1271,7 +1287,7 @@
         pltpu.SemaphoreType.DMA((reduce_sems(sizes, both),)),
         pltpu.SemaphoreType.DMA((2,)),
         pltpu.VMEM((n, piece, width), bf16),
-        pltpu.VMEM((count, piece, width), bf16),
+        pltpu.VMEM((count // hn, piece, width), bf16),
     ]
     if both:
         shapes.append(pltpu.VMEM((hn, fn, tn, 2, RANK, units), bf16))
@@ -1401,6 +1417,7 @@
     g_mid,
     sem,
     before_buf,
+    w_rows,
 ):
     i = pl.program_id(0)
     length = x_ref.shape[0]
@@ -1417,10 +1434,12 @@
 
     load_gh = pltpu.make_async_copy(gh_any, gh_buf, w_sems.at[3])
     load_before = pltpu.make_async_copy(before, before_buf, w_sems.at[5])
+    load_rows = pltpu.make_async_copy(w_any.at[:, :, pl.ds(width, RANK)], w_rows, w_sems.at[6])
     save = pltpu.make_async_copy(grads, a, w_sems.at[4])
 
     @pl.when(i == 0)
     def _():
+        load_rows.start()
         for j in range(3):
             load_w(j).start()
         load.start()
@@ -1429,12 +1448,11 @@
         enter_reduce(sizes, job.f, job.h, job.z)
         if grads.shape[0] > 6 * RANK:
             grads[6 * RANK :, :] = jnp.zeros((grads.shape[0] - 6 * RANK, width), bf16)
-        for j in range(3):
-            load_w(j).wait()
+        load_rows.wait()
 
         def small(j, _):
             m = sum(
-                nt(g_ref[j, :, p * half : (p + 1) * half], w_buf[j, p, pl.ds(width, RANK), :])
+                nt(g_ref[j, :, p * half : (p + 1) * half], w_rows[j, p])
                 for p in range(parts)
             ).astype(bf16)
             g_mid[j] = m
@@ -1460,6 +1478,7 @@
     @pl.when((i > 0) & (i < 4))
     def _():
         j = i - 1
+        load_w(j).wait()
         r = nn(g_mid[j], first_ref[j, number])
         for p in range(parts):
             r = r + nt(g_ref[j, :, p * half : (p + 1) * half], w_buf[j, p, pl.ds(0, width), :])
@@ -1515,7 +1534,7 @@
 def project_back(sizes, count, hot, index, before, g, w, first, mid, ln, gh, x, vectors):
     fn, hn, tn = sizes
     n, width = ln.shape
-    half = w.shape[-1]
+    parts, half = w.shape[1], w.shape[-1]
     length = x.shape[0]
     piece = piece_rows(6 * RANK, fn)
     any_ = pl.BlockSpec(memory_space=pl.ANY)
@@ -1549,7 +1568,7 @@
         + [
             pltpu.VMEM(w.shape, bf16),
             pltpu.VMEM((n, width), f32),
-            pltpu.SemaphoreType.DMA((6,)),
+            pltpu.SemaphoreType.DMA((7,)),
             pltpu.VMEM((n, width), f32),
             tail_shape(length, width),
             pltpu.VMEM((n, width), f32),
@@ -1557,10 +1576,69 @@
             pltpu.VMEM(mid.shape, bf16),
             pltpu.SemaphoreType.DMA((2,)),
             pltpu.VMEM(before.shape, bf16),
+            pltpu.VMEM((3, parts, RANK, half), bf16),
         ],
         compiler_params=params(collective_id=2, has_side_effects=True),
         name="qkv_back",
     )(hot, index, before, g, w, first, mid, ln, gh, x, vectors)
+
+
+def finish_kernel(count, last_any, *refs):
+    k = (len(refs) - 5) // 3
+    passed, outs = refs[:k], refs[k + 2 : 2 * k + 2]
+    g_in, g_out = refs[k : k + 2]
+    bufs, last_buf, sems, last_sem = refs[2 * k + 2 : 3 * k + 2], *refs[3 * k + 2 :]
+    load = pltpu.make_async_copy(last_any, last_buf, last_sem)
+    load.start()
+    moves = [Bounce(a, b, c, sems.at[i]) for i, (a, b, c) in enumerate(zip(passed, bufs, outs))]
+    for m in moves:
+        m.start()
+    load.wait()
+    piece, half = last_buf.shape[2], g_out.shape[-1]
+    h = lax.axis_index("heads")
+
+    def rows_of(j, r):
+        at = j * RANK + r * 8
+        return last_buf[at // piece, :, at % piece : at % piece + 8, :].astype(f32)
+
+    for m in moves:
+        m.turn()
+    for j in range(3):
+        for r in range(2):
+            g_in[j, :, r * 8 : r * 8 + 8, :] = rows_of(j, r)
+    for p in range(2):
+
+        @pl.when(h == p)
+        def _():
+            for j in range(3):
+                for r in range(2):
+                    g_out[j, :, r * 8 : r * 8 + 8, :] = rows_of(3 + j, r)[:, :, p * half : (p + 1) * half]
+
+    for m in moves:
+        m.wait()
+
+
+def finish(count, half, last, *passed):
+    width = last.shape[-1]
+    any_ = pl.BlockSpec(memory_space=pl.ANY)
+    vmem = pl.BlockSpec(memory_space=pltpu.VMEM)
+    shape = jax.ShapeDtypeStruct
+    k = len(passed)
+    return pl.pallas_call(
+        functools.partial(finish_kernel, count),
+        in_specs=[any_] * (k + 1),
+        out_specs=(vmem, vmem) + (any_,) * k,
+        out_shape=(shape((3, count, RANK, width), f32), shape((3, count, RANK, half), f32))
+        + tuple(shape(v.shape, v.dtype) for v in passed),
+        scratch_shapes=[pltpu.VMEM(v.shape, v.dtype) for v in passed]
+        + [
+            pltpu.VMEM(last.shape, bf16),
+            pltpu.SemaphoreType.DMA((k,)),
+            pltpu.SemaphoreType.DMA(()),
+        ],
+        compiler_params=params(),
+        name="finish",
+    )(last, *passed)
 
 
 def per_device(
@@ -1627,7 +1705,7 @@
     y, g_hidden, g_up_in, g_down_out, g_units, _ = mlp(
         sizes, ln2, cot, hidden, early, zw, ax, index, u_in, down_adapter_second, vectors
     )
-    g_mixed, grads = branch_back(
+    g_mixed, grads, y = branch_back(
         piece_rows(4 * RANK, fn) * fn,
         lambda: (lax.axis_index("fsdp") * hn + lax.axis_index("heads")) * tn + lax.axis_index("tensor"),
         index,
@@ -1638,6 +1716,7 @@
         proj_mid,
         g_up_in,
         g_down_out,
+        y,
     )
     by_place = image_adapter_index.reshape(fn, hn, tn)
     order = jnp.transpose(by_place, (2, 1, 0)).reshape(-1)
@@ -1662,14 +1741,14 @@
         x,
         vectors,
     )
-    last = jnp.moveaxis(last, 0, 1).reshape(count, -1, width)
-    last = jnp.moveaxis(last[:, : 6 * RANK].reshape(count, 6, RANK, width), 0, 1).astype(f32)
-    half = width // hn
+    g_qkv_in, g_qkv_out, g_x, g_proj_in, g_proj_out, g_up_in, g_up_out, g_down_in, g_down_out = finish(
+        count, width // hn, last, g_x, g_proj_in, g_proj_out, g_up_in, g_up_out, g_down_in, g_down_out
+    )
     return (
         jnp.swapaxes(y, 0, 1),
         jnp.swapaxes(g_x, 0, 1),
-        jnp.swapaxes(last[:3], 2, 3),
-        lax.dynamic_slice_in_dim(last[3:], h * half, half, axis=-1),
+        jnp.swapaxes(g_qkv_in, 2, 3),
+        g_qkv_out,
         jnp.swapaxes(g_proj_in, 1, 2),
         g_proj_out,
         jnp.swapaxes(g_up_in, 1, 2),

time: 326 us -> 319 us (0.979)
  local copies, waits for them, and re-layouts: 18.6 us -> 5.65 us
  Pallas kernels: 302 us -> 310 us
    unnamed x32 -> x6, local copies, waits for them, and re-layouts: 14.9 us -> 2.82 us
    pallas_call x0 -> x1, Pallas kernels: none -> 7.82 us  [finish(): pl.pallas_call(functools.partial(finish_kernel, count), in_specs=[any_] *...]
where the time goes in v2:
time: 319 us
  Pallas kernels  310 us (97%)
  local copies, waits for them, and re-layouts  5.65 us (2%)
    pallas_call x1, Pallas kernels, attention(): pl.pallas_call(functools.partial(attention_kernel, sizes), grid=(6 + head...  115 us
    pallas_call x1, Pallas kernels, mlp(): pl.pallas_call(functools.partial(mlp_kernel, sizes, length, done, plan),...  79.6 us
    pallas_call x1, Pallas kernels, attend_back(): pl.pallas_call(functools.partial(attend_back_kernel, sizes, length, count...  48.4 us
    pallas_call x1, Pallas kernels, project_back(): pl.pallas_call(functools.partial(project_back_kernel, sizes, count), grid...  48.3 us
    pallas_call x1, Pallas kernels, branch_back(): pl.pallas_call(functools.partial(branch_back_kernel, place), in_specs=[pl...  10.4 us
    pallas_call x1, Pallas kernels, finish(): pl.pallas_call(functools.partial(finish_kernel, count), in_specs=[any_] *...  7.82 us

profile of v2, /device:TPU:0, one launch (start us, length us, event | category | flops | bytes accessed | tf_op | source)
XLA Modules:
  0.0 318.7 jit_solution(13920638598075670432)
XLA Ops:
  0.7 0.7 constant_dynamic-update-slice_fusion.3
  1.4 0.7 constant_dynamic-update-slice_fusion.2
  2.1 0.7 constant_dynamic-update-slice_fusion.1
  2.8 0.7 constant_dynamic-update-slice_fusion
  3.5 0.7 convert_dynamic-update-slice_fusion
  4.2 0.6 reshape.71.vectors
  4.8 0.7 broadcast_in_dim.15
  5.5 0.6 pad.4.ub
  6.1 115.1 %attention.1 = (bf16[3,2,1168,576]{3,2,1,0:T(8,128)(2,1)}, bf16[2,1168,576]{2,1,0:T(8,128)(2,1)}, bf16[4,288,1076]{2,1,0:T(8,128)(2,1)}, bf16[2,4,32,1076]{3,2,1...) custom-call(bf16[3,288,576]{2,1,0:T(8,128)(2,1)} %bitcast.21, ...), custom_call_target="tpu_custom_call" | custom-call | tf_op jit(solution)/shard_map/attention/pallas_call | solution.py:701
  121.2 79.6 %mlp.1 = (f32[729,1,1152]{2,1,0:T(1,128)}, f32[736,1152]{1,0:T(8,128)}, bf16[16,1152]{1,0:T(8,128)(2,1)}, bf16[16,1152]{1,0:T(8,128)(2,1)}, bf16[2,4,16,1076]{3,...) custom-call(bf16[736,1184]{1,0:T(8,128)(2,1)} %get-tuple-element.50.ln_ref, ...), custom_call_target="tpu_custom_call", output_to_operand_aliasing={{5}: (3, {})} | custom-call | tf_op jit(solution)/shard_map/mlp/pallas_call | solution.py:930
  200.8 10.4 %branch_back.1 = (bf16[736,1152]{1,0:T(8,128)(2,1)}, bf16[64,1152]{1,0:T(8,128)(2,1)}, f32[729,1,1152]{2,1,0:T(1,128)}) custom-call(s32[32]{0:T(128)} %index.7, f32[736,1152]{1,0:T(8,128)} %get-tuple-element.55.gh_ref.gh_any, bf16[2,1168,576]{2,1,0:T(8,128)(2,1)} %get-tuple-element.56.w_ref, bf16[8,16,1152]{2,1,0:T(8,128)(2,1)} %out_bank.1, ...), custom_call_target="tpu_custom_call" | custom-call | tf_op jit(solution)/shard_map/branch_back/pallas_call | solution.py:1010
  211.3 0.1 mul.41
  211.4 0.1 copy.36
  211.5 0.1 mul.43
  211.7 0.1 mul.45
  211.9 0.8 fusion.1
  212.7 48.4 %attend_back.1 = (bf16[3,736,1152]{2,1,0:T(8,128)(2,1)}, bf16[4,8,16,1152]{3,2,1,0:T(8,128)(2,1)}, f32[8,16,1076]{2,1,0:T(8,128)}, f32[8,16,1076]{2,1,0:T(8,128)}) custom-call(bf16[128,512]{1,0:T(8,128)(2,1)} %get-tuple-element.92.hot, bf16[128,512]{1,0:T(8,128)(2,1)} %get-tuple-element.93.hot_b, bf16[3,736,1152]{2,1,0:T(8,128)(2,1)} %get-tuple-element.63.q_ref.k_ref.v_ref, ...), custom_call_target="tpu_custom_call" | custom-call | tf_op jit(solution)/shard_map/attend_back/pallas_call | solution.py:1356
  261.1 0.1 mul.37
  261.2 0.1 copy.35
  261.3 0.1 mul.39
  261.4 0.1 add.33
  261.5 0.8 fusion.hot
  262.3 48.3 %qkv_back.1 = (f32[729,1,1152]{2,1,0:T(1,128)}, bf16[4,8,24,1152]{3,2,1,0:T(8,128)(2,1)}, bf16[96,1152]{1,0:T(8,128)(2,1)}, f32[8,16,1152]{2,1,0:T(8,128)}, f32[...) custom-call(bf16[192,768]{1,0:T(8,128)(2,1)} %fusion.hot, s32[32]{0:T(128)} %index.7, ...), custom_call_target="tpu_custom_call" | custom-call | tf_op jit(solution)/shard_map/qkv_back/pallas_call | solution.py:1543
  310.7 7.8 %finish.1 = (f32[3,8,16,1152]{3,2,1,0:T(8,128)}, f32[3,8,16,576]{3,2,1,0:T(8,128)}, f32[729,1,1152]{2,1,0:T(1,128)}, f32[8,16,576]{2,1,0:T(8,128)}, f32[8,16,115...) custom-call(bf16[4,8,24,1152]{3,2,1,0:T(8,128)(2,1)} %get-tuple-elem, ...), custom_call_target="tpu_custom_call" | custom-call | tf_op jit(solution)/shard_map/finish/pallas_call | solution.py:1627
  (10 shorter events, 0.4 us)
Async XLA Ops:
  200.8 10.4 %copy-start = (s32[32]{0:T(128)S(1)}, s32[32]{0:T(128)}, u32[]{:S(2)}) copy-start(s32[32]{0:T(128)} %index.7) | copy-start | bytes 388

commit v3 on v2

--- a/solution.py
+++ b/solution.py
@@ -455,10 +455,10 @@
     ln_out,
     qkv_out,
     qmid_ref,
-    mixed_ref,
+    mixed_out,
     log_ref,
-    hidden_ref,
-    ln2_ref,
+    hidden_out,
+    ln2_out,
     mid_ref,
     got,
     send,
@@ -481,6 +481,9 @@
     x_buf,
     x_tail,
     x_sems,
+    mixed_ref,
+    hidden_ref,
+    ln2_ref,
 ):
     i = pl.program_id(0)
     fn, hn, tn = sizes
@@ -514,6 +517,10 @@
     load_q = lambda j: pltpu.make_async_copy(oq.at[j], wq_buf.at[j], w_sems.at[j])
     load_o = lambda: pltpu.make_async_copy(oo, wo_buf, w_sems.at[3])
     save_ln = lambda: pltpu.make_async_copy(lnx_ref.at[:, pl.ds(0, width)], ln_out, w_sems.at[4])
+    saves = [
+        pltpu.make_async_copy(a, b, w_sems.at[6 + k])
+        for k, (a, b) in enumerate(((mixed_ref, mixed_out), (hidden_ref, hidden_out), (ln2_ref, ln2_out)))
+    ]
     save_qkv = lambda: pltpu.make_async_copy(qkv_ref, qkv_out, w_sems.at[5])
 
     @pl.when(i == 0)
@@ -632,6 +639,7 @@
     @pl.when(i == 4 + heads)
     def _():
         to_lanes(mixed_ref, sum_ref)
+        saves[0].start()
         load_o().wait()
         br = sum(nt(mixed_ref[:, p * half : (p + 1) * half], wo_buf[p]) for p in range(hn))
         mid = br[:, width:].astype(bf16)
@@ -651,6 +659,8 @@
         lane = lax.broadcasted_iota(jnp.int32, (n, EXTRA - RANK), 1)
         ln2_ref[:, width : width + RANK] = up_mid.astype(bf16)
         ln2_ref[:, width + RANK :] = (lane == 0).astype(bf16)
+        saves[1].start()
+        saves[2].start()
         for b in blocks:
             b.exchange()
         save_qkv().wait()
@@ -667,6 +677,8 @@
             w.drain()
         for b in nxt:
             b.job.finish_first()
+        for c in saves:
+            c.wait()
 
 
 def attention(sizes, wq, wo, wu, wd, bq, bp, bu, bd, ub, index, first, out, x, vectors, up):
@@ -705,14 +717,14 @@
         + [one(v.shape) for v in (bq, bp, bu, bd, ub)]
         + [pl.BlockSpec(memory_space=pltpu.SMEM)]
         + [one(first.shape), one(out.shape), any_, one(vectors.shape), one(up.shape)],
-        out_specs=(any_,) * len(hbm) + tuple(one(s) for s, _ in outs) + (any_,),
+        out_specs=(any_,) * len(hbm) + tuple(any_ if k in (1, 3, 4) else one(s) for k, (s, _) in enumerate(outs)) + (any_,),
         out_shape=tuple(shape(*o) for o in hbm + outs) + (shape((tn, 2, width, units), bf16),),
         scratch_shapes=[
             pltpu.SemaphoreType.DMA((nsem,)),
             pltpu.SemaphoreType.DMA((nsem,)),
             pltpu.VMEM((3, hn, width + RANK, half), bf16),
             pltpu.VMEM((hn, width + RANK, half), bf16),
-            pltpu.SemaphoreType.DMA((6,)),
+            pltpu.SemaphoreType.DMA((9,)),
             pltpu.SemaphoreType.DMA((5, 2)),
             pltpu.VMEM((3, rows, half), bf16),
             pltpu.VMEM((rows, half), bf16),
@@ -728,6 +740,9 @@
             pltpu.VMEM((n, width), f32),
             tail_shape(length, width),
             pltpu.SemaphoreType.DMA((2,)),
+            pltpu.VMEM((n, width), bf16),
+            pltpu.VMEM((n, width), f32),
+            pltpu.VMEM((n, width + EXTRA), bf16),
         ],
         compiler_params=params(collective_id=3, has_side_effects=True),
         name="attention",
@@ -771,7 +786,7 @@
     plan,
     ln_ref,
     cot_ref,
-    hidden_ref,
+    hidden_any,
     early,
     zw,
     ax,
@@ -798,6 +813,8 @@
     g_acc,
     sem,
     own_buf,
+    hidden_ref,
+    hidden_sem,
 ):
     i = pl.program_id(0)
     fn, hn, tn = sizes
@@ -806,6 +823,7 @@
     number = index[(f * hn + h) * tn + z]
     gain, dbias = vectors.at[2:3], vectors.at[4:5]
     main = slice(0, width)
+    load_hidden = pltpu.make_async_copy(hidden_any, hidden_ref, hidden_sem)
     s, half = i // 2, lax.rem(i, 2)
     comm = Comm(send, recv)
     blocks = {b: Block(comm, sizes, zw, late.at[b], b, own_buf.at[b - done]) for b in range(done, tn)}
@@ -826,6 +844,7 @@
     def _():
         c = Tokens(cot_ref, g_buf, tail, sem)
         c.start()
+        load_hidden.start()
         for b in range(done):
             for w in loads(b):
                 w.start()
@@ -886,6 +905,8 @@
         g_down_out[...] = tn_(down_mid, gx[:, main]).astype(bf16)
         out_acc[:, main] += nn(down_mid, down_bank[number])
         g_acc[:, main] += nn(g_up_mid, up_bank[number])
+
+        load_hidden.wait()
 
         def body(rows, start):
             v = hidden_ref[rows, :]
@@ -933,7 +954,7 @@
         in_specs=[
             one((n, depth)),
             any_,
-            one((n, width)),
+            any_,
             any_,
             any_,
             any_,
@@ -973,6 +994,8 @@
             pltpu.VMEM((n, depth), f32),
             pltpu.SemaphoreType.DMA((2,)),
             pltpu.VMEM((late,) + zw.shape[1:], bf16),
+            pltpu.VMEM((n, width), f32),
+            pltpu.SemaphoreType.DMA(()),
         ],
         compiler_params=params(collective_id=4, has_side_effects=True),
         name="mlp",

time: 319 us -> 316 us (level)
  no operation moved by 1% of the time
where the time goes in v3:
time: 316 us
  Pallas kernels  307 us (97%)
  local copies, waits for them, and re-layouts  5.65 us (2%)
    pallas_call x1, Pallas kernels, attention(): pl.pallas_call(functools.partial(attention_kernel, sizes), grid=(6 + head...  113 us
    pallas_call x1, Pallas kernels, mlp(): pl.pallas_call(functools.partial(mlp_kernel, sizes, length, done, plan),...  78.6 us
    pallas_call x1, Pallas kernels, attend_back(): pl.pallas_call(functools.partial(attend_back_kernel, sizes, length, count...  48.4 us
    pallas_call x1, Pallas kernels, project_back(): pl.pallas_call(functools.partial(project_back_kernel, sizes, count), grid...  48.3 us
    pallas_call x1, Pallas kernels, branch_back(): pl.pallas_call(functools.partial(branch_back_kernel, place), in_specs=[pl...  10.4 us
    pallas_call x1, Pallas kernels, finish(): pl.pallas_call(functools.partial(finish_kernel, count), in_specs=[any_] *...  7.82 us

profile of v3, /device:TPU:0, one launch (start us, length us, event | category | flops | bytes accessed | tf_op | source)
XLA Modules:
  0.0 315.5 jit_solution(9605779868088834069)
XLA Ops:
  0.7 0.7 constant_dynamic-update-slice_fusion.3
  1.4 0.7 constant_dynamic-update-slice_fusion.2
  2.1 0.7 constant_dynamic-update-slice_fusion.1
  2.8 0.7 constant_dynamic-update-slice_fusion
  3.5 0.7 convert_dynamic-update-slice_fusion
  4.2 0.6 reshape.71.vectors
  4.8 0.7 broadcast_in_dim.15
  5.5 0.6 pad.4.ub
  6.1 113.0 %attention.1 = (bf16[3,2,1168,576]{3,2,1,0:T(8,128)(2,1)}, bf16[2,1168,576]{2,1,0:T(8,128)(2,1)}, bf16[4,288,1076]{2,1,0:T(8,128)(2,1)}, bf16[2,4,32,1076]{3,2,1...) custom-call(bf16[3,288,576]{2,1,0:T(8,128)(2,1)} %bitcast.21, ...), custom_call_target="tpu_custom_call" | custom-call | tf_op jit(solution)/shard_map/attention/pallas_call | solution.py:713
  119.1 78.6 %mlp.1 = (f32[729,1,1152]{2,1,0:T(1,128)}, f32[736,1152]{1,0:T(8,128)}, bf16[16,1152]{1,0:T(8,128)(2,1)}, bf16[16,1152]{1,0:T(8,128)(2,1)}, bf16[2,4,16,1076]{3,...) custom-call(bf16[736,1184]{1,0:T(8,128)(2,1)} %get-tuple-element.50.ln_ref, ...), custom_call_target="tpu_custom_call", output_to_operand_aliasing={{5}: (3, {})} | custom-call | tf_op jit(solution)/shard_map/mlp/pallas_call | solution.py:951
  197.7 10.4 %branch_back.1 = (bf16[736,1152]{1,0:T(8,128)(2,1)}, bf16[64,1152]{1,0:T(8,128)(2,1)}, f32[729,1,1152]{2,1,0:T(1,128)}) custom-call(s32[32]{0:T(128)} %index.7, f32[736,1152]{1,0:T(8,128)} %get-tuple-element.55.gh_ref.gh_any, bf16[2,1168,576]{2,1,0:T(8,128)(2,1)} %get-tuple-element.56.w_ref, bf16[8,16,1152]{2,1,0:T(8,128)(2,1)} %out_bank.1, ...), custom_call_target="tpu_custom_call" | custom-call | tf_op jit(solution)/shard_map/branch_back/pallas_call | solution.py:1033
  208.2 0.1 mul.41
  208.2 0.1 copy.36
  208.3 0.1 mul.43
  208.6 0.1 mul.45
  208.8 0.8 fusion.1
  209.6 48.4 %attend_back.1 = (bf16[3,736,1152]{2,1,0:T(8,128)(2,1)}, bf16[4,8,16,1152]{3,2,1,0:T(8,128)(2,1)}, f32[8,16,1076]{2,1,0:T(8,128)}, f32[8,16,1076]{2,1,0:T(8,128)}) custom-call(bf16[128,512]{1,0:T(8,128)(2,1)} %get-tuple-element.92.hot, bf16[128,512]{1,0:T(8,128)(2,1)} %get-tuple-element.93.hot_b, bf16[3,736,1152]{2,1,0:T(8,128)(2,1)} %get-tuple-element.63.q_ref.k_ref.v_ref, ...), custom_call_target="tpu_custom_call" | custom-call | tf_op jit(solution)/shard_map/attend_back/pallas_call | solution.py:1379
  258.0 0.1 mul.37
  258.1 0.1 copy.35
  258.2 0.1 mul.39
  258.4 0.1 add.33
  258.5 0.8 fusion.hot
  259.2 48.3 %qkv_back.1 = (f32[729,1,1152]{2,1,0:T(1,128)}, bf16[4,8,24,1152]{3,2,1,0:T(8,128)(2,1)}, bf16[96,1152]{1,0:T(8,128)(2,1)}, f32[8,16,1152]{2,1,0:T(8,128)}, f32[...) custom-call(bf16[192,768]{1,0:T(8,128)(2,1)} %fusion.hot, s32[32]{0:T(128)} %index.7, ...), custom_call_target="tpu_custom_call" | custom-call | tf_op jit(solution)/shard_map/qkv_back/pallas_call | solution.py:1566
  307.6 7.8 %finish.1 = (f32[3,8,16,1152]{3,2,1,0:T(8,128)}, f32[3,8,16,576]{3,2,1,0:T(8,128)}, f32[729,1,1152]{2,1,0:T(1,128)}, f32[8,16,576]{2,1,0:T(8,128)}, f32[8,16,115...) custom-call(bf16[4,8,24,1152]{3,2,1,0:T(8,128)(2,1)} %get-tuple-elem, ...), custom_call_target="tpu_custom_call" | custom-call | tf_op jit(solution)/shard_map/finish/pallas_call | solution.py:1650
  (10 shorter events, 0.4 us)
Async XLA Ops:
  197.7 10.4 %copy-start = (s32[32]{0:T(128)S(1)}, s32[32]{0:T(128)}, u32[]{:S(2)}) copy-start(s32[32]{0:T(128)} %index.7) | copy-start | bytes 388

commit v4 on v3

--- a/solution.py
+++ b/solution.py
@@ -795,7 +795,7 @@
     down_bank,
     vectors,
     y_ref,
-    gh_ref,
+    gh_out,
     g_up_in,
     g_down_out,
     g_units,
@@ -815,6 +815,7 @@
     own_buf,
     hidden_ref,
     hidden_sem,
+    gh_ref,
 ):
     i = pl.program_id(0)
     fn, hn, tn = sizes
@@ -916,11 +917,14 @@
             )
 
         by_rows(n, 32, body)
+        save = pltpu.make_async_copy(gh_ref, gh_out, hidden_sem)
+        save.start()
         c = Tokens(y_ref, out_acc, tail, sem, out=True)
         c.start()
         for b in blocks.values():
             b.drain()
         c.wait()
+        save.wait()
 
 
 def mlp(sizes, ln, cot, hidden, early, zw, ax, index, up, down, vectors):
@@ -965,7 +969,7 @@
         ],
         out_specs=(
             any_,
-            one((n, width)),
+            any_,
             one((RANK, width)),
             one((RANK, width)),
             one((2, tn, RANK, units)),
@@ -996,6 +1000,7 @@
             pltpu.VMEM((late,) + zw.shape[1:], bf16),
             pltpu.VMEM((n, width), f32),
             pltpu.SemaphoreType.DMA(()),
+            pltpu.VMEM((n, width), f32),
         ],
         compiler_params=params(collective_id=4, has_side_effects=True),
         name="mlp",

time: 316 us -> 316 us (level)
  no operation moved by 1% of the time
where the time goes in v4:
time: 316 us; the launch traced here: 315 us
  Pallas kernels  306 us (97%)
  local copies, waits for them, and re-layouts  5.65 us (2%)
    pallas_call x1, Pallas kernels, attention(): pl.pallas_call(functools.partial(attention_kernel, sizes), grid=(6 + head...  113 us
    pallas_call x1, Pallas kernels, mlp(): pl.pallas_call(functools.partial(mlp_kernel, sizes, length, done, plan),...  78.5 us
    pallas_call x1, Pallas kernels, attend_back(): pl.pallas_call(functools.partial(attend_back_kernel, sizes, length, count...  48.4 us
    pallas_call x1, Pallas kernels, project_back(): pl.pallas_call(functools.partial(project_back_kernel, sizes, count), grid...  48.3 us
    pallas_call x1, Pallas kernels, branch_back(): pl.pallas_call(functools.partial(branch_back_kernel, place), in_specs=[pl...  10.4 us
    pallas_call x1, Pallas kernels, finish(): pl.pallas_call(functools.partial(finish_kernel, count), in_specs=[any_] *...  7.82 us

profile of v4, /device:TPU:0, one launch (start us, length us, event | category | flops | bytes accessed | tf_op | source)
XLA Modules:
  0.0 315.5 jit_solution(3761833597752257324)
XLA Ops:
  0.7 0.7 constant_dynamic-update-slice_fusion.3
  1.4 0.7 constant_dynamic-update-slice_fusion.2
  2.1 0.7 constant_dynamic-update-slice_fusion.1
  2.8 0.7 constant_dynamic-update-slice_fusion
  3.5 0.7 convert_dynamic-update-slice_fusion
  4.2 0.6 reshape.71.vectors
  4.8 0.7 broadcast_in_dim.15
  5.5 0.6 pad.4.ub
  6.1 113.0 %attention.1 = (bf16[3,2,1168,576]{3,2,1,0:T(8,128)(2,1)}, bf16[2,1168,576]{2,1,0:T(8,128)(2,1)}, bf16[4,288,1076]{2,1,0:T(8,128)(2,1)}, bf16[2,4,32,1076]{3,2,1...) custom-call(bf16[3,288,576]{2,1,0:T(8,128)(2,1)} %bitcast.21, ...), custom_call_target="tpu_custom_call" | custom-call | tf_op jit(solution)/shard_map/attention/pallas_call | solution.py:713
  119.1 78.5 %mlp.1 = (f32[729,1,1152]{2,1,0:T(1,128)}, f32[736,1152]{1,0:T(8,128)}, bf16[16,1152]{1,0:T(8,128)(2,1)}, bf16[16,1152]{1,0:T(8,128)(2,1)}, bf16[2,4,16,1076]{3,...) custom-call(bf16[736,1184]{1,0:T(8,128)(2,1)} %get-tuple-element.50.ln_ref, ...), custom_call_target="tpu_custom_call", output_to_operand_aliasing={{5}: (3, {})} | custom-call | tf_op jit(solution)/shard_map/mlp/pallas_call | solution.py:955
  197.7 10.4 %branch_back.1 = (bf16[736,1152]{1,0:T(8,128)(2,1)}, bf16[64,1152]{1,0:T(8,128)(2,1)}, f32[729,1,1152]{2,1,0:T(1,128)}) custom-call(s32[32]{0:T(128)} %index.7, f32[736,1152]{1,0:T(8,128)} %get-tuple-element.55.gh_ref.gh_any, bf16[2,1168,576]{2,1,0:T(8,128)(2,1)} %get-tuple-element.56.w_ref, bf16[8,16,1152]{2,1,0:T(8,128)(2,1)} %out_bank.1, ...), custom_call_target="tpu_custom_call" | custom-call | tf_op jit(solution)/shard_map/branch_back/pallas_call | solution.py:1038
  208.1 0.1 mul.41
  208.2 0.1 copy.36
  208.3 0.1 mul.43
  208.5 0.1 mul.45
  208.8 0.8 fusion.1
  209.5 48.4 %attend_back.1 = (bf16[3,736,1152]{2,1,0:T(8,128)(2,1)}, bf16[4,8,16,1152]{3,2,1,0:T(8,128)(2,1)}, f32[8,16,1076]{2,1,0:T(8,128)}, f32[8,16,1076]{2,1,0:T(8,128)}) custom-call(bf16[128,512]{1,0:T(8,128)(2,1)} %get-tuple-element.92.hot, bf16[128,512]{1,0:T(8,128)(2,1)} %get-tuple-element.93.hot_b, bf16[3,736,1152]{2,1,0:T(8,128)(2,1)} %get-tuple-element.63.q_ref.k_ref.v_ref, ...), custom_call_target="tpu_custom_call" | custom-call | tf_op jit(solution)/shard_map/attend_back/pallas_call | solution.py:1384
  257.9 0.1 mul.37
  258.0 0.1 copy.35
  258.1 0.1 mul.39
  258.3 0.1 add.33
  258.4 0.8 fusion.hot
  259.1 48.3 %qkv_back.1 = (f32[729,1,1152]{2,1,0:T(1,128)}, bf16[4,8,24,1152]{3,2,1,0:T(8,128)(2,1)}, bf16[96,1152]{1,0:T(8,128)(2,1)}, f32[8,16,1152]{2,1,0:T(8,128)}, f32[...) custom-call(bf16[192,768]{1,0:T(8,128)(2,1)} %fusion.hot, s32[32]{0:T(128)} %index.7, ...), custom_call_target="tpu_custom_call" | custom-call | tf_op jit(solution)/shard_map/qkv_back/pallas_call | solution.py:1571
  307.5 7.8 %finish.1 = (f32[3,8,16,1152]{3,2,1,0:T(8,128)}, f32[3,8,16,576]{3,2,1,0:T(8,128)}, f32[729,1,1152]{2,1,0:T(1,128)}, f32[8,16,576]{2,1,0:T(8,128)}, f32[8,16,115...) custom-call(bf16[4,8,24,1152]{3,2,1,0:T(8,128)(2,1)} %get-tuple-elem, ...), custom_call_target="tpu_custom_call" | custom-call | tf_op jit(solution)/shard_map/finish/pallas_call | solution.py:1655
  (10 shorter events, 0.4 us)
Async XLA Ops:
  197.7 10.4 %copy-start = (s32[32]{0:T(128)S(1)}, s32[32]{0:T(128)}, u32[]{:S(2)}) copy-start(s32[32]{0:T(128)} %index.7) | copy-start | bytes 388
